TPU v7x, 32 devices: a whole 2x2x4 slice. The times are simulated.
32 devices in a mesh: dp: 8 (over z, y), tensor: 4 (over x, core).
Axes of the slice: x: 2, y: 2, z: 4, core: 2. Of those that a mesh axis runs over, the one named last changes fastest.
Arguments:
- tokens: bfloat16 [16384, 768], P('dp'), may hold values from -8 to 8
- lengths: int32 [8, 16], P('dp'), may hold values from 1 to 1024, 2048 in all within a row
- attn_gain: float32 [768], replicated, may hold values from 0.1 to 1.9
- qkv_weight: bfloat16 [768, 3, 768], P('dp', None, 'tensor'), may hold values from -0.21875 to 0.21875
- out_weight: bfloat16 [768, 768], P('tensor', 'dp'), may hold values from -0.625 to 0.625
- mlp_gain: float32 [768], replicated, may hold values from 0.1 to 1.9
- up_weight: bfloat16 [768, 2, 1152], P('dp', None, 'tensor'), may hold values from -0.21875 to 0.21875
- down_weight: bfloat16 [1152, 768], P('tensor', 'dp'), may hold values from -0.25 to 0.25
- cotangent: bfloat16 [16384, 768], P('dp'), may hold values from -8 to 8
Outputs:
- output: bfloat16 [16384, 768], P('dp')
- tokens_grad: float32 [16384, 768], P('dp')
- attn_gain_grad: float32 [768], P('dp')
- qkv_grad: float32 [768, 3, 768], P('dp', None, 'tensor')
- out_grad: float32 [768, 768], P('tensor', 'dp')
- mlp_gain_grad: float32 [768], P('dp')
- up_grad: float32 [768, 2, 1152], P('dp', None, 'tensor')
- down_grad: float32 [1152, 768], P('tensor', 'dp')
Inputs may be any that keep to these rules, and one draw needn't show every extreme that they name: Each row's 16 document lengths sum to 2048, and the longest of every row is exactly 1024.
All inputs are finite; a program needn't handle non-finite values.
Results may differ from a plain program's by a relative error of at most 0.02.
Values may be sent and summed in bfloat16 or wider, within the bound.
No kernel may reach another device: no remote copies, remote signals or barrier semaphores. Data moves between devices by JAX's collectives and lax.ppermute only.
A program may use at most 192 MiB of HBM per device.

v0:
```python
import math

import jax
import jax.numpy as jnp
from jax import lax
from jax.experimental import pallas as pl
from jax.experimental.pallas import tpu as pltpu
from jax.sharding import PartitionSpec as P

HD = 64

eps_norm = 1e-05
theta_base = 160000.0


def row_layout(row_lengths, tok_count):
    doc_ends = jnp.cumsum(row_lengths, dtype=jnp.int32)
    tok_place = jnp.arange(tok_count, dtype=jnp.int32)
    passed = tok_place[:, None] >= doc_ends[None, :]
    segment = jnp.sum(passed.astype(jnp.int32), axis=1, dtype=jnp.int32)
    doc_start = jnp.sum(jnp.where(passed, row_lengths[None, :], 0), axis=1, dtype=jnp.int32)
    return (segment, tok_place - doc_start)


def tile_ranges(row_lengths, tok_count):
    ends = jnp.cumsum(row_lengths, dtype=jnp.int32)
    starts = ends - row_lengths
    begin = jnp.arange(tok_count // TILE, dtype=jnp.int32)[:, None] * TILE
    touched = (ends[None, :] > begin) & (starts[None, :] < begin + TILE)
    low = jnp.min(jnp.where(touched, starts[None, :], tok_count), axis=1)
    high = jnp.max(jnp.where(touched, ends[None, :], 0), axis=1)
    return (low // TILE, (high + TILE - 1) // TILE)


def rotary_tables(position, head_width):
    half_width = head_width // 2
    freq_index = jnp.arange(half_width, dtype=jnp.float32)
    inv_freq = jnp.exp(freq_index * (-2.0 * math.log(theta_base) / head_width))
    angles = position.astype(jnp.float32)[:, None] * inv_freq[None, :]
    cosine, sine = jnp.cos(angles), jnp.sin(angles)
    return (jnp.concatenate([cosine, cosine], axis=1), jnp.concatenate([-sine, sine], axis=1))


def normalize(vector):
    row_mean = jnp.mean(vector, axis=-1, keepdims=True)
    centred = vector - row_mean
    spread = jnp.mean(centred * centred, axis=-1, keepdims=True)
    factor = lax.rsqrt(spread + eps_norm)
    return (centred * factor, factor)


def norm_back(grad_norm_out, normed, factor, gain_vec):
    grad_normed = grad_norm_out * gain_vec
    first_mean = jnp.mean(grad_normed, axis=-1, keepdims=True)
    second_mean = jnp.mean(grad_normed * normed, axis=-1, keepdims=True)
    return factor * (grad_normed - first_mean - normed * second_mean)


TILE = 256
NEG = -1e30


def nt_dot(a, b):
    return lax.dot_general(a, b, (((1,), (1,)), ((), ())), preferred_element_type=jnp.float32)


def nn_dot(a, b):
    return lax.dot_general(a, b, (((1,), (0,)), ((), ())), preferred_element_type=jnp.float32)


def tn_dot(a, b):
    return lax.dot_general(a, b, (((0,), (0,)), ((), ())), preferred_element_type=jnp.float32)


def swap_halves(u):
    half = u.shape[-1] // 2
    return jnp.concatenate([u[:, half:], u[:, :half]], axis=1)


def twice(a):
    return jnp.concatenate([a, a], axis=1)


def lane_fold(op, a):
    return op(a[:, : TILE // 2], a[:, TILE // 2 :])


def whole(shape):
    return pl.BlockSpec(shape, lambda *_: (0,) * len(shape))


def project_heads(h_one, weight, cos_tab, sin_tab, heads):
    tok_count, width = h_one.shape
    cols = heads * HD
    rows = 2 * TILE

    def body(h_ref, w_ref, c_ref, s_ref, q_ref, k_ref, v_ref):
        full = nn_dot(h_ref[...], w_ref[...])
        cosine, sine = c_ref[...], s_ref[...]
        for h in range(heads):
            u = full[:, h * HD : (h + 1) * HD]
            turned = (u * cosine + swap_halves(u) * sine).astype(jnp.bfloat16)
            q_ref[h] = (turned.astype(jnp.float32) * HD**-0.5).astype(jnp.bfloat16)
            u = full[:, cols + h * HD : cols + (h + 1) * HD]
            k_ref[h] = (u * cosine + swap_halves(u) * sine).astype(jnp.bfloat16)
            v_ref[h] = full[:, 2 * cols + h * HD : 2 * cols + (h + 1) * HD].astype(jnp.bfloat16)

    out = jax.ShapeDtypeStruct((heads, tok_count, HD), jnp.bfloat16)
    return pl.pallas_call(
        body,
        grid=(tok_count // rows,),
        in_specs=[
            pl.BlockSpec((rows, width), lambda i: (i, 0)),
            whole(weight.shape),
            pl.BlockSpec((rows, HD), lambda i: (i, 0)),
            pl.BlockSpec((rows, HD), lambda i: (i, 0)),
        ],
        out_specs=[pl.BlockSpec((heads, rows, HD), lambda i: (0, i, 0))] * 3,
        out_shape=[out] * 3,
        name="project_heads",
    )(h_one, weight, cos_tab, sin_tab)


def attend(first, last, place, query, key, value, seg_col, seg_row, parts):
    heads, tok_count, _ = query.shape
    blocks = tok_count // TILE
    share = blocks // parts
    half = TILE // 2

    def body(
        first_ref, last_ref, place_ref, q_ref, k_ref, v_ref, col_ref, row_ref, *refs
    ):
        low_refs, (out_ref, lse_ref, scores, peak, total, accum, low) = refs[:parts], refs[parts:]
        i = pl.program_id(0)
        lo, hi = first_ref[i], last_ref[i]
        peak[...] = jnp.full(peak.shape, NEG, jnp.float32)
        total[...] = jnp.zeros(total.shape, jnp.float32)
        accum[...] = jnp.zeros(accum.shape, jnp.float32)

        def score(j, carry):
            at = pl.multiple_of(j * TILE, TILE)
            same = twice(col_ref[...]) == row_ref[:, pl.ds(at, TILE)]
            for h in range(heads):
                s = jnp.where(same, nt_dot(q_ref[h], k_ref[h, pl.ds(at, TILE), :]), NEG)
                scores[h, j] = s
                peak[h] = jnp.maximum(peak[h], lane_fold(jnp.maximum, s))
            return carry

        lax.fori_loop(lo, hi, score, 0)
        for h in range(heads):
            peak[h] = jnp.broadcast_to(jnp.max(peak[h], axis=1, keepdims=True), (TILE, half))

        def spread(j, carry):
            at = pl.multiple_of(j * TILE, TILE)
            for h in range(heads):
                p = jnp.exp(scores[h, j] - twice(peak[h]))
                total[h] = total[h] + lane_fold(jnp.add, p)
                accum[h] = accum[h] + nn_dot(p.astype(jnp.bfloat16), v_ref[h, pl.ds(at, TILE), :])
            return carry

        lax.fori_loop(lo, hi, spread, 0)
        for h in range(heads):
            norm = jnp.sum(total[h], axis=1, keepdims=True)
            out = accum[h] / norm
            out_ref[h] = out
            low[:, h * HD : (h + 1) * HD] = out.astype(jnp.bfloat16)
            logs = peak[h] + jnp.log(jnp.broadcast_to(norm, (TILE, half)))
            lse_ref[h] = jnp.transpose(logs)[0:1, :]
        rows = pl.ds(pl.multiple_of((i % share) * TILE, TILE), TILE)
        for r in range(parts):

            @pl.when((i // share) ^ place_ref[0] == r)
            def _():
                low_refs[r][rows, :] = low[...]

    tile = pl.BlockSpec((heads, TILE, HD), lambda i, *_: (0, i, 0))
    return pl.pallas_call(
        body,
        grid_spec=pltpu.PrefetchScalarGridSpec(
            num_scalar_prefetch=3,
            grid=(blocks,),
            in_specs=[
                tile,
                whole(key.shape),
                whole(value.shape),
                pl.BlockSpec((TILE, half), lambda i, *_: (i, 0)),
                whole(seg_row.shape),
            ],
            out_specs=[whole((share * TILE, heads * HD))] * parts
            + [
                tile,
                pl.BlockSpec((heads, 1, TILE), lambda i, *_: (0, 0, i)),
            ],
            scratch_shapes=[
                pltpu.VMEM((heads, blocks, TILE, TILE), jnp.float32),
                pltpu.VMEM((heads, TILE, half), jnp.float32),
                pltpu.VMEM((heads, TILE, half), jnp.float32),
                pltpu.VMEM((heads, TILE, HD), jnp.float32),
                pltpu.VMEM((TILE, heads * HD), jnp.bfloat16),
            ],
        ),
        out_shape=[jax.ShapeDtypeStruct((share * TILE, heads * HD), jnp.bfloat16)] * parts
        + [
            jax.ShapeDtypeStruct((heads, tok_count, HD), jnp.float32),
            jax.ShapeDtypeStruct((heads, 1, tok_count), jnp.float32),
        ],
        name="attend",
    )(first, last, place, query, key, value, seg_col, seg_row)


def attend_grad(
    first, last, place, query, key, value, seg_col, seg_row, grads, out, lse, cos_tab, sin_tab
):
    heads, tok_count, _ = query.shape
    blocks = tok_count // TILE
    half = TILE // 2
    cols = heads * HD
    parts = len(grads)
    share = tok_count // parts

    def body(
        first_ref, last_ref, place_ref, q_ref, k_ref, v_ref, col_ref, row_ref, o_ref, lse_ref,
        c_ref, s_ref, *refs
    ):
        g_refs, (d_ref, split, inner, dq, dk, dv) = refs[:parts], refs[parts:]
        j = pl.program_id(0)
        lo, hi = first_ref[j], last_ref[j]
        here = pl.ds(pl.multiple_of(j * TILE, TILE), TILE)

        @pl.when(j == 0)
        def _():
            dq[...] = jnp.zeros(dq.shape, jnp.float32)
            for b in range(blocks):
                r, off = b * TILE // share, b * TILE % share
                base = (place_ref[0] ^ r) * share + off
                rows = pl.ds(pl.multiple_of(base, TILE), TILE)
                for h in range(heads):
                    g = g_refs[r][off : off + TILE, h * HD : (h + 1) * HD]
                    split[h, rows, :] = g
                    dots = jnp.sum(g.astype(jnp.float32) * o_ref[h, rows, :], axis=1, keepdims=True)
                    dots = jnp.transpose(jnp.broadcast_to(dots, (TILE, half)))
                    inner[h, :, rows] = dots[0:1, :]

        dk[...] = jnp.zeros(dk.shape, jnp.float32)
        dv[...] = jnp.zeros(dv.shape, jnp.float32)

        def step(i, carry):
            at = pl.ds(pl.multiple_of(i * TILE, TILE), TILE)
            same = twice(col_ref[...]) == row_ref[:, at]
            for h in range(heads):
                q, g, k = q_ref[h, at, :], split[h, at, :], k_ref[h, here, :]
                s = jnp.where(same, nt_dot(k, q), NEG)
                p = jnp.exp(s - lse_ref[h, :, at])
                dp = nt_dot(v_ref[h, here, :], g)
                ds = (p * (dp - inner[h, :, at])).astype(jnp.bfloat16)
                dv[h] = dv[h] + nn_dot(p.astype(jnp.bfloat16), g)
                dk[h] = dk[h] + nn_dot(ds, q)
                dq[h, at, :] = dq[h, at, :] + tn_dot(ds, k)
            return carry

        lax.fori_loop(lo, hi, step, 0)
        cosine, sine = c_ref[here, :], s_ref[here, :]
        for h in range(heads):
            w = dk[h]
            w = (w * cosine - swap_halves(w) * sine).astype(jnp.bfloat16)
            d_ref[here, cols + h * HD : cols + (h + 1) * HD] = w
            d_ref[here, 2 * cols + h * HD : 2 * cols + (h + 1) * HD] = dv[h].astype(jnp.bfloat16)

        @pl.when(j == blocks - 1)
        def _():
            for b in range(blocks):
                rows = slice(b * TILE, (b + 1) * TILE)
                for h in range(heads):
                    w = dq[h, rows, :] * HD**-0.5
                    w = w * c_ref[rows, :] - swap_halves(w) * s_ref[rows, :]
                    d_ref[rows, h * HD : (h + 1) * HD] = w.astype(jnp.bfloat16)

    return pl.pallas_call(
        body,
        grid_spec=pltpu.PrefetchScalarGridSpec(
            num_scalar_prefetch=3,
            grid=(blocks,),
            in_specs=[
                whole(query.shape),
                whole(key.shape),
                whole(value.shape),
                pl.BlockSpec((TILE, half), lambda i, *_: (i, 0)),
                whole(seg_row.shape),
                whole(out.shape),
                whole(lse.shape),
                whole(cos_tab.shape),
                whole(sin_tab.shape),
            ]
            + [whole(g.shape) for g in grads],
            out_specs=whole((tok_count, 3 * cols)),
            scratch_shapes=[
                pltpu.VMEM((heads, tok_count, HD), jnp.bfloat16),
                pltpu.VMEM((heads, 1, tok_count), jnp.float32),
                pltpu.VMEM((heads, tok_count, HD), jnp.float32),
                pltpu.VMEM((heads, TILE, HD), jnp.float32),
                pltpu.VMEM((heads, TILE, HD), jnp.float32),
            ],
        ),
        out_shape=jax.ShapeDtypeStruct((tok_count, 3 * cols), jnp.bfloat16),
        name="attend_grad",
    )(first, last, place, query, key, value, seg_col, seg_row, out, lse, cos_tab, sin_tab, *grads)


def swap(value, axis, step):
    count = lax.axis_size(axis)
    return lax.ppermute(value, axis, [(i, i ^ step) for i in range(count)])


def gather_far(shard):
    return [shard] + [swap(shard, "dp", step) for step in range(2, lax.axis_size("dp"), 2)]


def gather_near(pieces):
    return [v for piece in pieces for v in (piece, swap(piece, "dp", 1))]


def assemble(pieces, place, kind=None):
    count = len(pieces)
    lead, (rows, cols) = pieces[0].shape[:-2], pieces[0].shape[-2:]
    if rows % 16:
        order = place[0] ^ jnp.arange(count, dtype=jnp.int32)
        ranked = jnp.take(jnp.stack(pieces), order, axis=0)
        return jnp.moveaxis(ranked, 0, -3).reshape(*lead, count * rows, cols)

    kind = kind or pieces[0].dtype

    def body(place_ref, *refs):
        for r in range(count):
            at = pl.ds(pl.multiple_of((place_ref[0] ^ r) * rows, 16), rows)
            refs[count][(slice(None),) * len(lead) + (at, slice(None))] = refs[r][...].astype(kind)

    return pl.pallas_call(
        body,
        grid_spec=pltpu.PrefetchScalarGridSpec(
            num_scalar_prefetch=1,
            grid=(1,),
            in_specs=[whole(pieces[0].shape)] * count,
            out_specs=whole((*lead, count * rows, cols)),
        ),
        out_shape=jax.ShapeDtypeStruct((*lead, count * rows, cols), kind),
        name="assemble",
    )(place, *pieces)


def reduce_near(total, place):
    count = lax.axis_size("dp")
    rows, cols = total.shape[0] // count, total.shape[1]
    order = place[0] ^ jnp.array([*range(0, count, 2), *range(1, count, 2)], jnp.int32)
    ranked = jnp.take(total.reshape(count, rows, cols), order, axis=0)
    return ranked[: count // 2], swap(ranked[count // 2 :], "dp", 1)


def reduce_far(near, come):
    near = near.astype(jnp.float32) + come.astype(jnp.float32)
    low = near.astype(jnp.bfloat16)
    result = near[0]
    for slot in range(1, near.shape[0]):
        result = result + swap(low[slot], "dp", 2 * slot).astype(jnp.float32)
    return result


def layer(
    att, source, cot, gain, weight_near, weight_far, hid
):
    tok_count, width = source.shape
    head_cols = att[0].shape[1]
    parts = len(att)
    ff = parts * hid
    inner = parts * head_cols
    rows = 256

    def body(*refs):
        a_refs = refs[:parts]
        x_ref, c_ref, g_ref, wa_ref, wb_ref = refs[parts : parts + 5]
        out_ref, dmid_ref, dlow_ref, h_ref, hid_ref, dg_ref, dv_ref, gg_ref = refs[
            parts + 5 : parts + 13
        ]
        d_refs = refs[parts + 13 : 2 * parts + 13]
        gate, lift, down, proj = refs[2 * parts + 13 :]

        @pl.when(pl.program_id(0) == 0)
        def _():
            gg_ref[...] = jnp.zeros(gg_ref.shape, jnp.float32)
            for slot in range(parts):
                w_ref, s = (wa_ref, wb_ref)[slot // 2], slot % 2
                at = slice(slot * hid, (slot + 1) * hid)
                gate[:, at] = w_ref[s, :, :hid]
                lift[:, at] = w_ref[s, :, hid : 2 * hid]
                down[:, at] = w_ref[s, :, 2 * hid : 3 * hid]
                proj[:, slot * head_cols : (slot + 1) * head_cols] = w_ref[
                    s, :, 3 * hid : 3 * hid + head_cols
                ]

        gain_vec = g_ref[...]
        attended = jnp.concatenate([a_refs[r][...] for r in SLOTS], axis=1)
        mid = x_ref[...].astype(jnp.float32) + nt_dot(attended, proj[...])
        normed, factor = normalize(mid)
        h_two = (normed * gain_vec).astype(jnp.bfloat16)
        h_ref[...] = h_two
        cot_low = c_ref[...]
        first = nn_dot(h_two, gate[...])
        second = nn_dot(h_two, lift[...])
        below = 0.5 * (1.0 + lax.erf(first * math.sqrt(0.5)))
        active = first * below
        hidden = (active * second).astype(jnp.bfloat16)
        hid_ref[...] = hidden
        out_ref[...] = (mid + nt_dot(hidden, down[...])).astype(jnp.bfloat16)
        slope = below + first * (jnp.exp(-0.5 * first * first) * (1.0 / math.sqrt(2.0 * math.pi)))
        d_hidden = nn_dot(cot_low, down[...]).astype(jnp.bfloat16).astype(jnp.float32)
        d_first = (d_hidden * second * slope).astype(jnp.bfloat16)
        d_second = (d_hidden * active).astype(jnp.bfloat16)
        dg_ref[...] = d_first
        dv_ref[...] = d_second
        d_h = nt_dot(d_first, gate[...]) + nt_dot(d_second, lift[...])
        gg_ref[...] += jnp.sum(d_h * normed, axis=0, keepdims=True)
        d_mid = cot_low.astype(jnp.float32) + norm_back(d_h, normed, factor, gain_vec)
        dmid_ref[...] = d_mid
        d_low = d_mid.astype(jnp.bfloat16)
        dlow_ref[...] = d_low
        d_att = nn_dot(d_low, proj[...]).astype(jnp.bfloat16)
        for slot in range(parts):
            d_refs[SLOTS[slot]][...] = d_att[:, slot * head_cols : (slot + 1) * head_cols]

    def tile(cols):
        return pl.BlockSpec((rows, cols), lambda i: (i, 0))

    def fixed(shape):
        return pl.BlockSpec(shape, lambda *_: (0,) * len(shape), pipeline_mode=pl.Buffered(1))

    def shape(cols, kind=jnp.bfloat16):
        return jax.ShapeDtypeStruct((tok_count, cols), kind)

    return pl.pallas_call(
        body,
        grid=(tok_count // rows,),
        in_specs=[tile(head_cols)] * parts
        + [tile(width), tile(width), whole((1, width))]
        + [fixed(weight_near.shape), fixed(weight_far.shape)],
        out_specs=[tile(width)] * 4
        + [tile(ff)] * 3
        + [whole((1, width))]
        + [tile(head_cols)] * parts,
        out_shape=[
            shape(width),
            shape(width, jnp.float32),
            shape(width),
            shape(width),
            shape(ff),
            shape(ff),
            shape(ff),
            jax.ShapeDtypeStruct((1, width), jnp.float32),
        ]
        + [shape(head_cols)] * parts,
        scratch_shapes=[
            pltpu.VMEM((width, ff), jnp.bfloat16),
            pltpu.VMEM((width, ff), jnp.bfloat16),
            pltpu.VMEM((width, ff), jnp.bfloat16),
            pltpu.VMEM((width, inner), jnp.bfloat16),
        ],
        name="layer",
    )(*att, source, cot, gain[None, :], weight_near, weight_far)


SLOTS = (0, 2, 1, 3)


def weight_grads(side, h_two, d_first, d_second, cot, hidden, d_low, att, gain_grad, wide):
    _, width = h_two.shape
    hid = hidden.shape[1] // len(SLOTS)
    head_cols = att[0].shape[1]
    both = tuple(att[r] for r in SLOTS[2 * side : 2 * side + 2])
    here = slice(2 * side * hid, (2 * side + 2) * hid)

    def body(h_ref, f_ref, s_ref, c_ref, u_ref, l_ref, a_ref, b_ref, g_ref, out_ref):
        for ref, turned, at in ((f_ref, h_ref, 0), (s_ref, h_ref, hid), (u_ref, c_ref, 2 * hid)):
            full = tn_dot(turned[...], ref[:, here]).astype(jnp.bfloat16)
            out_ref[0, :, at : at + hid] = full[:, :hid]
            out_ref[1, :, at : at + hid] = full[:, hid:]
        gain_col = jnp.transpose(jnp.broadcast_to(g_ref[...], (128, width))).astype(jnp.bfloat16)
        for s, ref in ((0, a_ref), (1, b_ref)):
            at = 3 * hid
            out_ref[s, :, at : at + head_cols] = tn_dot(l_ref[...], ref[...]).astype(jnp.bfloat16)
            out_ref[s, :, at + head_cols :] = gain_col[:, : wide - at - head_cols]

    return pl.pallas_call(
        body,
        out_shape=jax.ShapeDtypeStruct((2, width, wide), jnp.bfloat16),
        name="weight_grads",
    )(h_two, d_first, d_second, cot, hidden, d_low, *both, gain_grad)


def back_to_width(d_qkv, weight, place, slots, share):
    width, cols = weight.shape
    first, stride = slots[0], slots[1] - slots[0]

    def body(place_ref, d_ref, w_ref, out_ref):
        out_ref[0] = nt_dot(d_ref[...], w_ref[...]).astype(jnp.bfloat16)

    return pl.pallas_call(
        body,
        grid_spec=pltpu.PrefetchScalarGridSpec(
            num_scalar_prefetch=1,
            grid=(len(slots),),
            in_specs=[
                pl.BlockSpec((share, cols), lambda i, at: (at[0] ^ (first + stride * i), 0)),
                whole(weight.shape),
            ],
            out_specs=pl.BlockSpec((1, share, width), lambda i, at: (i, 0, 0)),
        ),
        out_shape=jax.ShapeDtypeStruct((len(slots), share, width), jnp.bfloat16),
        name="back_to_width",
    )(place, d_qkv, weight)


def share_rows(mine, place, kind=None):
    other = swap(mine, "tensor", 2)
    far = swap(jnp.stack([mine, other]), "tensor", 1)
    return assemble([mine, far[0], other, far[1]], place, kind)


def layer_shards(
    tokens, lengths, attn_gain, qkv_weight, out_weight, mlp_gain, up_weight, down_weight, cotangent
):
    tok_count, _ = tokens.shape
    parts = lax.axis_size("tensor")
    share = tok_count // parts
    rank = lax.axis_index("tensor").astype(jnp.int32)
    place = rank[None]
    dp_place = lax.axis_index("dp").astype(jnp.int32)[None]
    rows = qkv_weight.shape[0]
    head_cols = qkv_weight.shape[2]
    heads_dev = head_cols // HD
    hid = up_weight.shape[2]
    used = 3 * hid + head_cols
    wide = used // 128 * 128 + 128

    qkv_own = qkv_weight.reshape(rows, 3 * head_cols)
    qkv_own, up_weight, down_weight, out_weight = lax.optimization_barrier(
        (qkv_own, up_weight, down_weight, out_weight)
    )
    qkv_far = gather_far(qkv_own)
    qkv_flat = assemble(gather_near(qkv_far), dp_place)
    packed = jnp.concatenate(
        [
            up_weight.reshape(rows, 2 * hid),
            down_weight.T,
            out_weight.T,
            jnp.zeros((rows, wide - used), jnp.bfloat16),
        ],
        axis=1,
    )
    paired = jnp.stack([packed, swap(packed, "tensor", 2)])
    paired, _ = lax.optimization_barrier((paired, qkv_far))
    paired_far = gather_far(paired)

    segment, position = row_layout(lengths[0], tok_count)
    cosine, sine_table = rotary_tables(position, HD)
    h_one = (normalize(tokens.astype(jnp.float32))[0] * attn_gain).astype(jnp.bfloat16)
    seg_col = jnp.broadcast_to(segment[:, None], (tok_count, TILE // 2))
    seg_row = segment[None, :]
    first, last = tile_ranges(lengths[0], tok_count)
    query, key, value = project_heads(h_one, qkv_flat, cosine, sine_table, heads_dev)
    paired_far, query = lax.optimization_barrier((paired_far, query))
    pieces = gather_near(paired_far)
    *sent, attended_wide, log_total = attend(
        first, last, place, query, key, value, seg_col, seg_row, parts
    )
    sent, pieces = lax.optimization_barrier((sent, pieces))
    weight_near = assemble(pieces, dp_place)
    weight_far = swap(weight_near, "tensor", 1)
    att = [sent[0]] + [swap(sent[r], "tensor", r) for r in range(1, parts)]
    my_tokens = lax.dynamic_slice_in_dim(tokens, rank * share, share, 0)
    my_cot = lax.dynamic_slice_in_dim(cotangent, rank * share, share, 0)
    out, d_mid, d_low, h_two, hidden, d_first, d_second, gain_two, *d_sent = layer(
        att, my_tokens, my_cot, mlp_gain, weight_near, weight_far, hid
    )
    d_att = [d_sent[0]] + [swap(d_sent[r], "tensor", r) for r in range(1, parts)]
    output = share_rows(out, place)

    grads_in = (h_two, d_first, d_second, my_cot, hidden, d_low, att, gain_two, wide)
    grads_far = weight_grads(1, *grads_in)
    grads_near = weight_grads(0, *grads_in)
    chip = grads_near.astype(jnp.float32) + swap(grads_far, "tensor", 1).astype(jnp.float32)
    chip_sent, d_att = lax.optimization_barrier((chip[1].astype(jnp.bfloat16), d_att))
    column_come = swap(chip_sent, "tensor", 2)

    d_qkv = attend_grad(
        first,
        last,
        place,
        query,
        key,
        value,
        seg_col,
        seg_row,
        d_att,
        attended_wide,
        log_total,
        cosine,
        sine_table,
    )
    d_far = back_to_width(d_qkv, qkv_flat, place, (1, 3), share)
    d_near = back_to_width(d_qkv, qkv_flat, place, (0, 2), share)
    d_chip = d_near.astype(jnp.float32) + swap(d_far, "tensor", 1).astype(jnp.float32)
    d_sent, d_qkv, column_come = lax.optimization_barrier(
        (d_chip[1].astype(jnp.bfloat16), d_qkv, column_come)
    )
    d_come = swap(d_sent, "tensor", 2)
    column = (chip[0] + column_come.astype(jnp.float32)).astype(jnp.bfloat16)
    column_near, column_come = reduce_near(column, dp_place)
    qkv_total = jnp.einsum("td,tf->df", h_one, d_qkv, preferred_element_type=jnp.float32)
    qkv_near, qkv_come = reduce_near(qkv_total.astype(jnp.bfloat16), dp_place)
    normed_one, factor_one = normalize(my_tokens.astype(jnp.float32))
    d_h_one = d_chip[0] + d_come.astype(jnp.float32)
    tokens_grad = d_mid + norm_back(d_h_one, normed_one, factor_one, attn_gain)
    tokens_grad, column_come, qkv_come = lax.optimization_barrier(
        (tokens_grad.astype(jnp.bfloat16), column_come, qkv_come)
    )
    tokens_grad = share_rows(tokens_grad, place, jnp.float32)
    reduced = reduce_far(column_near, column_come)
    up_grad = reduced[:, : 2 * hid].reshape(rows, 2, hid)
    down_grad = reduced[:, 2 * hid : 3 * hid].T
    out_grad = reduced[:, 3 * hid : used].T
    mlp_gain_grad = reduced[:, used]
    qkv_grad = reduce_far(qkv_near, qkv_come)
    gain_one = jnp.sum(qkv_grad * qkv_own.astype(jnp.float32), axis=1)
    gain_one = gain_one + sum(swap(gain_one, "tensor", r) for r in range(1, parts))
    attn_gain_grad = gain_one / lax.dynamic_slice_in_dim(attn_gain, dp_place[0] * rows, rows, 0)
    qkv_grad = qkv_grad.reshape(rows, 3, head_cols)
    return (
        output,
        tokens_grad,
        attn_gain_grad,
        qkv_grad,
        out_grad,
        mlp_gain_grad,
        up_grad,
        down_grad,
    )


def solution(mesh):
    in_specs = (
        P("dp", None),
        P("dp", None),
        P(),
        P("dp", None, "tensor"),
        P("tensor", "dp"),
        P(),
        P("dp", None, "tensor"),
        P("tensor", "dp"),
        P("dp", None),
    )
    out_specs = (
        P("dp", None),
        P("dp", None),
        P("dp"),
        P("dp", None, "tensor"),
        P("tensor", "dp"),
        P("dp"),
        P("dp", None, "tensor"),
        P("tensor", "dp"),
    )
    return jax.shard_map(layer_shards, mesh=mesh, in_specs=in_specs, out_specs=out_specs, check_vma=False)
```

profile of v0, /device:TPU:0, one launch (start us, length us, event | category | flops | bytes accessed | tf_op | source)
XLA Modules:
  0.0 384.5 jit_solution(6940819324233974829)
XLA Ops:
  2.0 5.1 %collective-permute-start.3 = (bf16[96,576]{1,0:T(8,128)(2,1)S(1)}, bf16[96,576]{1,0:T(8,128)(2,1)}, u32[]{:S(2)}, u32[]{:S(2)}) collective-permute-start(bf16[96,576]{1,0:T(8,128)(2,1)S(1)} %copy.73.refs_0_), channel_id=1, source_target_pairs={{0,24},{4,28},{8,16},{12,20},{16,8},{20,12},{24,0},{28,4},{1,25},{... | collective-permute-start | bytes 331784 | tf_op jit(solution)/shard_map/ppermute | solution.py:311
  25.0 3.7 fusion.24
  31.8 2.9 collective-permute-start.5
  39.1 3.2 collective-permute-done.10.refs_7_
  44.7 2.8 collective-permute-done.9.refs_5_
  49.8 8.2 %project_heads.1 = (bf16[3,2048,64]{2,1,0:T(8,128)(2,1)}, bf16[3,2048,64]{2,1,0:T(8,128)(2,1)}, bf16[3,2048,64]{2,1,0:T(8,128)(2,1)}) custom-call(bf16[2048,768]{1,0:T(8,128)(2,1)} %fusion.4.h_ref, bf16[768,576]{1,0:T(8,128)(2,1)} %assemble.4.w_ref, f32[2048,64]{1,0:T(8,128)} %get-tuple-element.187.c_ref, f32[2048,64]{1,0:T(8,128)} %get-tuple-element.188.s_ref), custom_call_target="tpu_custom_call" | custom-call | tf_op jit(solution)/shard_map/project_heads/pallas_call | solution.py:109
  58.0 7.1 %collective-permute-done.5.refs_4_ = bf16[2,96,1152]{2,1,0:T(8,128)(2,1)} collective-permute-done((bf16[2,96,1152]{2,1,0:T(8,128)(2,1)}, bf16[2,96,1152]{2,1,0:T(8,128)(2,1)}, u32[]{:S(2)}, u32[]{:S(2)}) %collective-permute-start.5) | collective-permute-done | bytes 442400 | tf_op jit(solution)/shard_map/ppermute | solution.py:311
  71.2 28.7 %attend.1 = (bf16[512,192]{1,0:T(8,128)(2,1)}, bf16[512,192]{1,0:T(8,128)(2,1)}, bf16[512,192]{1,0:T(8,128)(2,1)}, bf16[512,192]{1,0:T(8,128)(2,1)}, f32[3,2048,64]{2,1,0:T(8,128)}, /*index=5*/f32[3,1,2048]{2,1,0:T(1,128)}) custom-call(s32[8]{0:T(128)} %get-tuple-element.186.first_ref, s32[8]{0:T(128)} %get-tuple-element.185.last_ref, s32[1]{0:T(128)} %bitcast.place_ref, ...), custom_call_target="tpu_custom_call" | custom-call | tf_op jit(solution)/shard_map/attend/pallas_call | solution.py:177
  100.9 4.0 %assemble.5.refs_7_ = bf16[2,768,1152]{2,1,0:T(8,128)(2,1)} custom-call(s32[1]{0:T(128)} %bitcast.8.place_ref, bf16[2,96,1152]{2,1,0:T(8,128)(2,1)} %pad_maximum_fusion.4.refs_0_, bf16[2,96,1152]{2,1,0:T(8,128)(2,1)} %collective-permute-done.11.refs_1_, bf16[2,96,1152]{2,1,0:T(8,128)(2,1)} %collective-permute-done.4.refs_2_, ...), custom_call_target="tpu_custom_call" | custom-call | tf_op jit(solution)/shard_map/assemble/pallas_call | solution.py:337
  111.8 3.1 collective-permute-done.16.refs_2_.b_ref
  114.9 3.7 collective-permute-done.17.refs_3_.b_ref
  119.2 19.6 %layer.1 = (bf16[512,768]{1,0:T(8,128)(2,1)}, f32[512,768]{1,0:T(8,128)}, bf16[512,768]{1,0:T(8,128)(2,1)}, bf16[512,768]{1,0:T(8,128)(2,1)}, bf16[512,1152]{1,0...) custom-call(bf16[512,192]{1,0:T(8,128)(2,1)} %get-tuple-element.79.r, ...), custom_call_target="tpu_custom_call" | custom-call | tf_op jit(solution)/shard_map/layer/pallas_call | solution.py:438
  138.9 8.2 %weight_grads.3 = bf16[2,768,1152]{2,1,0:T(8,128)(2,1)} custom-call(bf16[512,768]{1,0:T(8,128)(2,1)} %get-tuple-element.95.h_ref, bf16[512,1152]{1,0:T(8,128)(2,1)} %get-tuple-element.96.f_ref, bf16[512,1152]{1,0:T(8,128)(2,1)} %get-tuple-element.97.s_ref, bf16[512,768]{1,0:T(8,128)(2,1)} %constant_dynamic-slice_fusion.refs_5_.c_ref, ...), custom_call_target="tpu_custom_call" | custom-call | tf_op jit(solution)/shard_map/weight_grads/pallas_call | solution.py:490
  150.3 7.2 %weight_grads.2 = bf16[2,768,1152]{2,1,0:T(8,128)(2,1)} custom-call(bf16[512,768]{1,0:T(8,128)(2,1)} %get-tuple-element.95.h_ref, bf16[512,1152]{1,0:T(8,128)(2,1)} %get-tuple-element.96.f_ref, bf16[512,1152]{1,0:T(8,128)(2,1)} %get-tuple-element.97.s_ref, bf16[512,768]{1,0:T(8,128)(2,1)} %constant_dynamic-slice_fusion.refs_5_.c_ref, ...), custom_call_target="tpu_custom_call" | custom-call | tf_op jit(solution)/shard_map/weight_grads/pallas_call | solution.py:490
  157.5 10.8 %collective-permute-done.19.refs_2_ = bf16[512,768]{1,0:T(8,128)(2,1)S(1)} collective-permute-done((bf16[512,768]{1,0:T(8,128)(2,1)S(1)}, bf16[512,768]{1,0:T(8,128)(2,1)S(1)}, u32[]{:S(2)}, u32[]{:S(2)}) %collective-permute-start.19) | collective-permute-done | bytes 786464 | tf_op jit(solution)/shard_map/ppermute | solution.py:311
  169.7 3.8 convert_add_fusion
  173.5 2.8 copy-done.4
  178.6 56.0 %attend_grad.1.d_ref = bf16[2048,576]{1,0:T(8,128)(2,1)} custom-call(s32[8]{0:T(128)} %get-tuple-element.186.first_ref, s32[8]{0:T(128)} %get-tuple-element.185.last_ref, s32[1]{0:T(128)} %bitcast.place_ref, bf16[3,2048,64]{2,1,0:T(8,128)(2,1)} %get-tuple-element.68.q_ref, bf16[3,2048,64]{2,1,0:T(8,128)(2,1)} %get-tuple-element.69.k_ref, ...), custom_call_target="tpu_custom_call" | custom-call | tf_op jit(solution)/shard_map/attend_grad/pallas_call | solution.py:278
  234.6 4.0 %back_to_width.3 = bf16[2,512,768]{2,1,0:T(8,128)(2,1)} custom-call(s32[1]{0:T(128)} %bitcast.place_ref, bf16[2048,576]{1,0:T(8,128)(2,1)} %attend_grad.1.d_ref, bf16[768,576]{1,0:T(8,128)(2,1)} %assemble.4.w_ref), custom_call_target="tpu_custom_call" | custom-call | tf_op jit(solution)/shard_map/back_to_width/pallas_call | solution.py:504
  242.8 3.7 assemble.6
  246.5 3.9 %back_to_width.2 = bf16[2,512,768]{2,1,0:T(8,128)(2,1)} custom-call(s32[1]{0:T(128)} %bitcast.place_ref, bf16[2048,576]{1,0:T(8,128)(2,1)} %attend_grad.1.d_ref, bf16[768,576]{1,0:T(8,128)(2,1)} %assemble.4.w_ref), custom_call_target="tpu_custom_call" | custom-call | tf_op jit(solution)/shard_map/back_to_width/pallas_call | solution.py:504
  253.7 26.3 %collective-permute-done.26 = bf16[768,1152]{1,0:T(8,128)(2,1)} collective-permute-done((bf16[768,1152]{1,0:T(8,128)(2,1)}, bf16[768,1152]{1,0:T(8,128)(2,1)}, u32[]{:S(2)}, u32[]{:S(2)}) %collective-permute-start.26) | collective-permute-done | bytes 1769504 | tf_op jit(solution)/shard_map/ppermute | solution.py:311
  280.0 4.1 %fusion.6 = bf16[768,1152]{1,0:T(8,128)(2,1)} fusion(f32[2,768,1152]{2,1,0:T(8,128)} %copy-done.4, bf16[768,1152]{1,0:T(8,128)(2,1)} %collective-permute-done.26), kind=kLoop, calls=%fused_computation.12 | loop fusion | flops 2654208 | bytes 7077888 | tf_op jit(solution)/shard_map/convert_element_type | solution.py:614
  284.1 3.5 gather_fusion
  292.2 4.9 %convolution_convert_fusion = bf16[768,576]{0,1:T(8,128)(2,1)} fusion(bf16[2048,768]{1,0:T(8,128)(2,1)} %fusion.4.h_ref, bf16[2048,576]{1,0:T(8,128)(2,1)S(1)} %copy-done.3), kind=kOutput, calls=%fused_computation.38 | convolution fusion | flops 1812381696 | bytes 6389760 | tf_op jit(solution)/shard_map/td,tf->df/dot_general | solution.py:616
  304.2 6.4 %collective-permute-done.27 = bf16[512,768]{1,0:T(8,128)(2,1)} collective-permute-done((bf16[512,768]{1,0:T(8,128)(2,1)}, bf16[512,768]{1,0:T(8,128)(2,1)}, u32[]{:S(2)}, u32[]{:S(2)}) %collective-permute-start.27) | collective-permute-done | bytes 786464 | tf_op jit(solution)/shard_map/ppermute | solution.py:311
  314.7 8.4 %collective-permute-done.29 = bf16[4,96,576]{2,1,0:T(8,128)(2,1)S(1)} collective-permute-done((bf16[4,96,576]{2,1,0:T(8,128)(2,1)S(1)}, bf16[4,96,576]{2,1,0:T(8,128)(2,1)S(1)}, u32[]{:S(2)}, u32[]{:S(2)}) %collective-permute-start.29) | collective-permute-done | bytes 442400 | tf_op jit(solution)/shard_map/ppermute | solution.py:311
  323.9 8.0 %collective-permute-start.32 = (bf16[96,576]{1,0:T(8,128)(2,1)S(1)}, bf16[96,576]{1,0:T(8,128)(2,1)S(1)}, u32[]{:S(2)}, u32[]{:S(2)}) collective-permute-start(bf16[96,576]{1,0:T(8,128)(2,1)S(1)} %get-tuple-element.179), channel_id=1, source_target_pairs={{0,8},{4,12},{8,0},{12,4},{16,24},{20,28},{24,16},{28,20},{1,9},{5... | collective-permute-start | bytes 331784 | tf_op jit(solution)/shard_map/ppermute | solution.py:311
  336.9 4.1 %collective-permute-done.30.refs_2_ = bf16[512,768]{1,0:T(8,128)(2,1)S(1)} collective-permute-done((bf16[512,768]{1,0:T(8,128)(2,1)S(1)}, bf16[512,768]{1,0:T(8,128)(2,1)S(1)}, u32[]{:S(2)}, u32[]{:S(2)}) %collective-permute-start.30) | collective-permute-done | bytes 786464 | tf_op jit(solution)/shard_map/ppermute | solution.py:311
  343.2 8.0 %collective-permute-start.38 = (bf16[96,1152]{1,0:T(8,128)(2,1)S(1)}, bf16[96,1152]{1,0:T(8,128)(2,1)S(1)}, u32[]{:S(2)}, u32[]{:S(2)}) collective-permute-start(bf16[96,1152]{1,0:T(8,128)(2,1)S(1)} %get-tuple-element.176), channel_id=1, source_target_pairs={{0,8},{4,12},{8,0},{12,4},{16,24},{20,28},{24,16},{28,20},{1,9},{5... | collective-permute-start | bytes 663560 | tf_op jit(solution)/shard_map/ppermute | solution.py:311
  357.7 14.3 %collective-permute-done.39 = bf16[96,1152]{1,0:T(8,128)(2,1)S(1)} collective-permute-done((bf16[96,1152]{1,0:T(8,128)(2,1)S(1)}, bf16[96,1152]{1,0:T(8,128)(2,1)S(1)}, u32[]{:S(2)}, u32[]{:S(2)}) %collective-permute-start.39) | collective-permute-done | bytes 221216 | tf_op jit(solution)/shard_map/ppermute | solution.py:311
  379.1 5.1 %assemble.7 = f32[2048,768]{1,0:T(8,128)} custom-call(s32[1]{0:T(128)} %bitcast.place_ref, bf16[512,768]{1,0:T(8,128)(2,1)} %copy-done.9, bf16[512,768]{1,0:T(8,128)(2,1)} %get-tuple-element.171.refs_1_, bf16[512,768]{1,0:T(8,128)(2,1)} %copy-done.12, bf16[512,768]{1,0:T(8,128)(2,1)} %get-tuple-element.170.refs_3_), custom_call_target="tpu_custom_call" | custom-call | tf_op jit(solution)/shard_map/assemble/pallas_call | solution.py:337
  (202 shorter events, 97.6 us)
Async XLA Ops:
  2.0 28.5 %collective-permute-start.3 = (bf16[96,576]{1,0:T(8,128)(2,1)S(1)}, bf16[96,576]{1,0:T(8,128)(2,1)}, u32[]{:S(2)}, u32[]{:S(2)}) collective-permute-start(bf16[96,576]{1,0:T(8,128)(2,1)S(1)} %copy.73.refs_0_), channel_id=1, source_target_pairs={{0,24},{4,28},{8,16},{12,20},{16,8},{20,12},{24,0},{28,4},{1,25},{... | collective-permute-start | bytes 331784 | tf_op jit(solution)/shard_map/ppermute | solution.py:311
  7.2 23.3 %collective-permute-start.1 = (bf16[96,576]{1,0:T(8,128)(2,1)S(1)}, bf16[96,576]{1,0:T(8,128)(2,1)}, u32[]{:S(2)}, u32[]{:S(2)}) collective-permute-start(bf16[96,576]{1,0:T(8,128)(2,1)S(1)} %copy.73.refs_0_), channel_id=1, source_target_pairs={{0,8},{4,12},{8,0},{12,4},{16,24},{20,28},{24,16},{28,20},{1,9},{5... | collective-permute-start | bytes 331784 | tf_op jit(solution)/shard_map/ppermute | solution.py:311
  7.2 23.3 %collective-permute-start.2 = (bf16[96,576]{1,0:T(8,128)(2,1)S(1)}, bf16[96,576]{1,0:T(8,128)(2,1)}, u32[]{:S(2)}, u32[]{:S(2)}) collective-permute-start(bf16[96,576]{1,0:T(8,128)(2,1)S(1)} %copy.73.refs_0_), channel_id=1, source_target_pairs={{0,16},{4,20},{8,24},{12,28},{16,0},{20,4},{24,8},{28,12},{1,17},{... | collective-permute-start | bytes 331784 | tf_op jit(solution)/shard_map/ppermute | solution.py:311
  7.8 29.6 %collective-permute-start.7 = (bf16[96,576]{1,0:T(8,128)(2,1)S(1)}, bf16[96,576]{1,0:T(8,128)(2,1)}, u32[]{:S(2)}, u32[]{:S(2)}) collective-permute-start(bf16[96,576]{1,0:T(8,128)(2,1)S(1)} %copy.73.refs_0_), channel_id=1, source_target_pairs={{0,4},{4,0},{8,12},{12,8},{16,20},{20,16},{24,28},{28,24},{1,5},{5... | collective-permute-start | bytes 331784 | tf_op jit(solution)/shard_map/ppermute | solution.py:311
  15.4 13.3 %collective-permute-start = (bf16[96,1152]{1,0:T(8,128)(2,1)S(1)}, bf16[96,1152]{1,0:T(8,128)(2,1)}, u32[]{:S(2)}, u32[]{:S(2)}) collective-permute-start(bf16[96,1152]{1,0:T(8,128)(2,1)S(1)} %concatenate.9), channel_id=1, source_target_pairs={{0,2},{1,3},{2,0},{3,1},{4,6},{5,7},{6,4},{7,5},{8,10},{9,11},{10,... | collective-permute-start | bytes 663560 | tf_op jit(solution)/shard_map/ppermute | solution.py:311
  30.5 27.4 %collective-permute-start.4 = (bf16[2,96,1152]{2,1,0:T(8,128)(2,1)}, bf16[2,96,1152]{2,1,0:T(8,128)(2,1)}, u32[]{:S(2)}, u32[]{:S(2)}) collective-permute-start(bf16[2,96,1152]{2,1,0:T(8,128)(2,1)} %pad_maximum_fusion.4.refs_0_), channel_id=1, source_target_pairs={{0,8},{4,12},{8,0},{12,4},{16,24},{20,28},{24,16},{28,20},{1,9},{5... | collective-permute-start | bytes 1327112 | tf_op jit(solution)/shard_map/ppermute | solution.py:311
  31.8 33.2 %collective-permute-start.5 = (bf16[2,96,1152]{2,1,0:T(8,128)(2,1)}, bf16[2,96,1152]{2,1,0:T(8,128)(2,1)}, u32[]{:S(2)}, u32[]{:S(2)}) collective-permute-start(bf16[2,96,1152]{2,1,0:T(8,128)(2,1)} %pad_maximum_fusion.4.refs_0_), channel_id=1, source_target_pairs={{0,16},{4,20},{8,24},{12,28},{16,0},{20,4},{24,8},{28,12},{1,17},{... | collective-permute-start | bytes 1327112 | tf_op jit(solution)/shard_map/ppermute | solution.py:311
  34.7 30.3 %collective-permute-start.6 = (bf16[2,96,1152]{2,1,0:T(8,128)(2,1)}, bf16[2,96,1152]{2,1,0:T(8,128)(2,1)}, u32[]{:S(2)}, u32[]{:S(2)}) collective-permute-start(bf16[2,96,1152]{2,1,0:T(8,128)(2,1)} %pad_maximum_fusion.4.refs_0_), channel_id=1, source_target_pairs={{0,24},{4,28},{8,16},{12,20},{16,8},{20,12},{24,0},{28,4},{1,25},{... | collective-permute-start | bytes 1327112 | tf_op jit(solution)/shard_map/ppermute | solution.py:311
  65.1 34.8 %collective-permute-start.11 = (bf16[2,96,1152]{2,1,0:T(8,128)(2,1)}, bf16[2,96,1152]{2,1,0:T(8,128)(2,1)}, u32[]{:S(2)}, u32[]{:S(2)}) collective-permute-start(bf16[2,96,1152]{2,1,0:T(8,128)(2,1)} %pad_maximum_fusion.4.refs_0_), channel_id=1, source_target_pairs={{0,4},{4,0},{8,12},{12,8},{16,20},{20,16},{24,28},{28,24},{1,5},{5... | collective-permute-start | bytes 1327112 | tf_op jit(solution)/shard_map/ppermute | solution.py:311
  65.6 34.3 %collective-permute-start.12 = (bf16[2,96,1152]{2,1,0:T(8,128)(2,1)}, bf16[2,96,1152]{2,1,0:T(8,128)(2,1)}, u32[]{:S(2)}, u32[]{:S(2)}) collective-permute-start(bf16[2,96,1152]{2,1,0:T(8,128)(2,1)} %collective-permute-done.4.refs_2_), channel_id=1, source_target_pairs={{0,4},{4,0},{8,12},{12,8},{16,20},{20,16},{24,28},{28,24},{1,5},{5... | collective-permute-start | bytes 1327112 | tf_op jit(solution)/shard_map/ppermute | solution.py:311
  67.1 32.8 %collective-permute-start.13 = (bf16[2,96,1152]{2,1,0:T(8,128)(2,1)}, bf16[2,96,1152]{2,1,0:T(8,128)(2,1)}, u32[]{:S(2)}, u32[]{:S(2)}) collective-permute-start(bf16[2,96,1152]{2,1,0:T(8,128)(2,1)} %collective-permute-done.5.refs_4_), channel_id=1, source_target_pairs={{0,4},{4,0},{8,12},{12,8},{16,20},{20,16},{24,28},{28,24},{1,5},{5... | collective-permute-start | bytes 1327112 | tf_op jit(solution)/shard_map/ppermute | solution.py:311
  67.6 33.3 %collective-permute-start.14 = (bf16[2,96,1152]{2,1,0:T(8,128)(2,1)}, bf16[2,96,1152]{2,1,0:T(8,128)(2,1)}, u32[]{:S(2)}, u32[]{:S(2)}) collective-permute-start(bf16[2,96,1152]{2,1,0:T(8,128)(2,1)} %collective-permute-done.6.refs_6_), channel_id=1, source_target_pairs={{0,4},{4,0},{8,12},{12,8},{16,20},{20,16},{24,28},{28,24},{1,5},{5... | collective-permute-start | bytes 1327112 | tf_op jit(solution)/shard_map/ppermute | solution.py:311
  105.0 14.3 %collective-permute-start.18 = (bf16[2,768,1152]{2,1,0:T(8,128)(2,1)}, bf16[2,768,1152]{2,1,0:T(8,128)(2,1)}, u32[]{:S(2)}, u32[]{:S(2)}) collective-permute-start(bf16[2,768,1152]{2,1,0:T(8,128)(2,1)} %assemble.5.refs_7_), channel_id=1, source_target_pairs={{0,1},{1,0},{2,3},{3,2},{4,5},{5,4},{6,7},{7,6},{8,9},{9,8},{10,11... | collective-permute-start | bytes 10616840 | tf_op jit(solution)/shard_map/ppermute | solution.py:311
  106.0 12.5 %collective-permute-start.17 = (bf16[512,192]{1,0:T(8,128)(2,1)}, bf16[512,192]{1,0:T(8,128)(2,1)S(1)}, u32[]{:S(2)}, u32[]{:S(2)}) collective-permute-start(bf16[512,192]{1,0:T(8,128)(2,1)} %get-tuple-element.82), channel_id=1, source_target_pairs={{0,3},{1,2},{2,1},{3,0},{4,7},{5,6},{6,5},{7,4},{8,11},{9,10},{10,... | collective-permute-start | bytes 589832 | tf_op jit(solution)/shard_map/ppermute | solution.py:311
  147.1 22.6 %collective-permute-start.21 = (bf16[2,768,1152]{2,1,0:T(8,128)(2,1)}, bf16[2,768,1152]{2,1,0:T(8,128)(2,1)}, u32[]{:S(2)}, u32[]{:S(2)}) collective-permute-start(bf16[2,768,1152]{2,1,0:T(8,128)(2,1)} %weight_grads.3), channel_id=1, source_target_pairs={{0,1},{1,0},{2,3},{3,2},{4,5},{5,4},{6,7},{7,6},{8,9},{9,8},{10,11... | collective-permute-start | bytes 10616840 | tf_op jit(solution)/shard_map/ppermute | solution.py:311
  147.9 20.4 %collective-permute-start.19 = (bf16[512,768]{1,0:T(8,128)(2,1)S(1)}, bf16[512,768]{1,0:T(8,128)(2,1)S(1)}, u32[]{:S(2)}, u32[]{:S(2)}) collective-permute-start(bf16[512,768]{1,0:T(8,128)(2,1)S(1)} %copy-done.13), channel_id=1, source_target_pairs={{0,2},{1,3},{2,0},{3,1},{4,6},{5,7},{6,4},{7,5},{8,10},{9,11},{10,... | collective-permute-start | bytes 2359304 | tf_op jit(solution)/shard_map/ppermute | solution.py:311
  148.4 29.3 %collective-permute-start.22 = (bf16[512,192]{1,0:T(8,128)(2,1)S(1)}, bf16[512,192]{1,0:T(8,128)(2,1)S(1)}, u32[]{:S(2)}, u32[]{:S(2)}) collective-permute-start(bf16[512,192]{1,0:T(8,128)(2,1)S(1)} %copy-done.33), channel_id=1, source_target_pairs={{0,1},{1,0},{2,3},{3,2},{4,5},{5,4},{6,7},{7,6},{8,9},{9,8},{10,11... | collective-permute-start | bytes 589832 | tf_op jit(solution)/shard_map/ppermute | solution.py:311
  148.4 29.3 %collective-permute-start.23 = (bf16[512,192]{1,0:T(8,128)(2,1)S(1)}, bf16[512,192]{1,0:T(8,128)(2,1)S(1)}, u32[]{:S(2)}, u32[]{:S(2)}) collective-permute-start(bf16[512,192]{1,0:T(8,128)(2,1)S(1)} %copy-done.32), channel_id=1, source_target_pairs={{0,2},{1,3},{2,0},{3,1},{4,6},{5,7},{6,4},{7,5},{8,10},{9,11},{10,... | collective-permute-start | bytes 589832 | tf_op jit(solution)/shard_map/ppermute | solution.py:311
  150.0 27.7 %collective-permute-start.24 = (bf16[512,192]{1,0:T(8,128)(2,1)S(1)}, bf16[512,192]{1,0:T(8,128)(2,1)S(1)}, u32[]{:S(2)}, u32[]{:S(2)}) collective-permute-start(bf16[512,192]{1,0:T(8,128)(2,1)S(1)} %copy-done.31), channel_id=1, source_target_pairs={{0,3},{1,2},{2,1},{3,0},{4,7},{5,6},{6,5},{7,4},{8,11},{9,10},{10,... | collective-permute-start | bytes 589832 | tf_op jit(solution)/shard_map/ppermute | solution.py:311
  169.7 70.4 %collective-permute-start.20 = (bf16[2,512,768]{2,1,0:T(8,128)(2,1)}, bf16[2,512,768]{2,1,0:T(8,128)(2,1)}, u32[]{:S(2)}, u32[]{:S(2)}) collective-permute-start(bf16[2,512,768]{2,1,0:T(8,128)(2,1)} %pad_maximum_fusion), channel_id=1, source_target_pairs={{0,1},{1,0},{2,3},{3,2},{4,5},{5,4},{6,7},{7,6},{8,9},{9,8},{10,11... | collective-permute-start | bytes 4718600 | tf_op jit(solution)/shard_map/ppermute | solution.py:311
  238.6 11.8 %collective-permute-start.25 = (bf16[2,512,768]{2,1,0:T(8,128)(2,1)}, bf16[2,512,768]{2,1,0:T(8,128)(2,1)}, u32[]{:S(2)}, u32[]{:S(2)}) collective-permute-start(bf16[2,512,768]{2,1,0:T(8,128)(2,1)} %back_to_width.3), channel_id=1, source_target_pairs={{0,1},{1,0},{2,3},{3,2},{4,5},{5,4},{6,7},{7,6},{8,9},{9,8},{10,11... | collective-permute-start | bytes 4718600 | tf_op jit(solution)/shard_map/ppermute | solution.py:311
  239.2 40.8 %collective-permute-start.26 = (bf16[768,1152]{1,0:T(8,128)(2,1)}, bf16[768,1152]{1,0:T(8,128)(2,1)}, u32[]{:S(2)}, u32[]{:S(2)}) collective-permute-start(bf16[768,1152]{1,0:T(8,128)(2,1)} %fusion.11), channel_id=1, source_target_pairs={{0,2},{1,3},{2,0},{3,1},{4,6},{5,7},{6,4},{7,5},{8,10},{9,11},{10,... | collective-permute-start | bytes 5308424 | tf_op jit(solution)/shard_map/ppermute | solution.py:311
  291.7 31.4 %collective-permute-start.28 = (bf16[4,96,1152]{2,1,0:T(8,128)(2,1)}, bf16[4,96,1152]{2,1,0:T(8,128)(2,1)}, u32[]{:S(2)}, u32[]{:S(2)}) collective-permute-start(bf16[4,96,1152]{2,1,0:T(8,128)(2,1)} %slice.108), channel_id=1, source_target_pairs={{0,4},{4,0},{8,12},{12,8},{16,20},{20,16},{24,28},{28,24},{1,5},{5... | collective-permute-start | bytes 2654216 | tf_op jit(solution)/shard_map/ppermute | solution.py:311
  291.7 18.9 %collective-permute-start.27 = (bf16[512,768]{1,0:T(8,128)(2,1)}, bf16[512,768]{1,0:T(8,128)(2,1)}, u32[]{:S(2)}, u32[]{:S(2)}) collective-permute-start(bf16[512,768]{1,0:T(8,128)(2,1)} %fusion.20), channel_id=1, source_target_pairs={{0,2},{1,3},{2,0},{3,1},{4,6},{5,7},{6,4},{7,5},{8,10},{9,11},{10,... | collective-permute-start | bytes 2359304 | tf_op jit(solution)/shard_map/ppermute | solution.py:311
  302.1 21.0 %collective-permute-start.29 = (bf16[4,96,576]{2,1,0:T(8,128)(2,1)S(1)}, bf16[4,96,576]{2,1,0:T(8,128)(2,1)S(1)}, u32[]{:S(2)}, u32[]{:S(2)}) collective-permute-start(bf16[4,96,576]{2,1,0:T(8,128)(2,1)S(1)} %slice.109), channel_id=1, source_target_pairs={{0,4},{4,0},{8,12},{12,8},{16,20},{20,16},{24,28},{28,24},{1,5},{5... | collective-permute-start | bytes 1327112 | tf_op jit(solution)/shard_map/ppermute | solution.py:311
  323.2 17.8 %collective-permute-start.30 = (bf16[512,768]{1,0:T(8,128)(2,1)S(1)}, bf16[512,768]{1,0:T(8,128)(2,1)S(1)}, u32[]{:S(2)}, u32[]{:S(2)}) collective-permute-start(bf16[512,768]{1,0:T(8,128)(2,1)S(1)} %fusion.16.refs_0_), channel_id=1, source_target_pairs={{0,2},{1,3},{2,0},{3,1},{4,6},{5,7},{6,4},{7,5},{8,10},{9,11},{10,... | collective-permute-start | bytes 2359304 | tf_op jit(solution)/shard_map/ppermute | solution.py:311
  323.9 18.6 %collective-permute-start.32 = (bf16[96,576]{1,0:T(8,128)(2,1)S(1)}, bf16[96,576]{1,0:T(8,128)(2,1)S(1)}, u32[]{:S(2)}, u32[]{:S(2)}) collective-permute-start(bf16[96,576]{1,0:T(8,128)(2,1)S(1)} %get-tuple-element.179), channel_id=1, source_target_pairs={{0,8},{4,12},{8,0},{12,4},{16,24},{20,28},{24,16},{28,20},{1,9},{5... | collective-permute-start | bytes 331784 | tf_op jit(solution)/shard_map/ppermute | solution.py:311
  342.3 34.1 %collective-permute-start.31 = (bf16[2,512,768]{2,1,0:T(8,128)(2,1)}, bf16[2,512,768]{2,1,0:T(8,128)(2,1)}, u32[]{:S(2)}, u32[]{:S(2)}) collective-permute-start(bf16[2,512,768]{2,1,0:T(8,128)(2,1)} %pad_maximum_fusion.1), channel_id=1, source_target_pairs={{0,1},{1,0},{2,3},{3,2},{4,5},{5,4},{6,7},{7,6},{8,9},{9,8},{10,11... | collective-permute-start | bytes 4718600 | tf_op jit(solution)/shard_map/ppermute | solution.py:311
  342.6 10.7 %collective-permute-start.35 = (f32[96]{0:T(128)S(1)}, f32[96]{0:T(128)S(1)}, u32[]{:S(2)}, u32[]{:S(2)}) collective-permute-start(f32[96]{0:T(128)S(1)} %get-tuple-element.162), channel_id=1, source_target_pairs={{0,1},{1,0},{2,3},{3,2},{4,5},{5,4},{6,7},{7,6},{8,9},{9,8},{10,11... | collective-permute-start | bytes 1160 | tf_op jit(solution)/shard_map/ppermute | solution.py:311
  343.2 14.5 %collective-permute-start.38 = (bf16[96,1152]{1,0:T(8,128)(2,1)S(1)}, bf16[96,1152]{1,0:T(8,128)(2,1)S(1)}, u32[]{:S(2)}, u32[]{:S(2)}) collective-permute-start(bf16[96,1152]{1,0:T(8,128)(2,1)S(1)} %get-tuple-element.176), channel_id=1, source_target_pairs={{0,8},{4,12},{8,0},{12,4},{16,24},{20,28},{24,16},{28,20},{1,9},{5... | collective-permute-start | bytes 663560 | tf_op jit(solution)/shard_map/ppermute | solution.py:311
  353.3 18.7 %collective-permute-start.39 = (bf16[96,1152]{1,0:T(8,128)(2,1)S(1)}, bf16[96,1152]{1,0:T(8,128)(2,1)S(1)}, u32[]{:S(2)}, u32[]{:S(2)}) collective-permute-start(bf16[96,1152]{1,0:T(8,128)(2,1)S(1)} %get-tuple-element.178), channel_id=1, source_target_pairs={{0,16},{4,20},{8,24},{12,28},{16,0},{20,4},{24,8},{28,12},{1,17},{... | collective-permute-start | bytes 663560 | tf_op jit(solution)/shard_map/ppermute | solution.py:311
  355.0 17.0 %collective-permute-start.40 = (bf16[96,1152]{1,0:T(8,128)(2,1)S(1)}, bf16[96,1152]{1,0:T(8,128)(2,1)S(1)}, u32[]{:S(2)}, u32[]{:S(2)}) collective-permute-start(bf16[96,1152]{1,0:T(8,128)(2,1)S(1)} %get-tuple-element.177), channel_id=1, source_target_pairs={{0,24},{4,28},{8,16},{12,20},{16,8},{20,12},{24,0},{28,4},{1,25},{... | collective-permute-start | bytes 663560 | tf_op jit(solution)/shard_map/ppermute | solution.py:311
  (43 other events, 457.9 us)
where the time goes:
time: 390 us; the launch traced here: 384 us
  Pallas kernels  151 us (39%)
  waiting for transfers between devices  94.4 us (24%)
  starting transfers between devices  53.3 us (14%)
  other arithmetic  42.7 us (11%)
  local copies, waits for them, and re-layouts  36.7 us (9%)
  matrix products  4.85 us (1%)
    ppermute x41, waiting for transfers between devices, swap(): return lax.ppermute(value, axis, [(i, i ^ step) for i in range(count)])  94.4 us
    pallas_call x1, Pallas kernels, attend_grad(): pl.pallas_call(body, grid_spec=pltpu.PrefetchScalarGridSpec(num_scalar_pr...  56 us
    ppermute x41, starting transfers between devices, swap(): return lax.ppermute(value, axis, [(i, i ^ step) for i in range(count)])  53.3 us
    pallas_call x1, Pallas kernels, attend(): pl.pallas_call(body, grid_spec=pltpu.PrefetchScalarGridSpec(num_scalar_pr...  28.7 us
    pallas_call x1, Pallas kernels, layer(): pl.pallas_call(body, grid=(tok_count // rows,), in_specs=[tile(head_cols)...  19.6 us
    pallas_call x2, Pallas kernels, weight_grads(): pl.pallas_call(body, out_shape=jax.ShapeDtypeStruct((2, width, wide), jnp...  15.4 us
    pallas_call x4, Pallas kernels, assemble(): pl.pallas_call(body, grid_spec=pltpu.PrefetchScalarGridSpec(num_scalar_pr...  15.1 us
    unnamed x72, local copies, waits for them, and re-layouts  9.41 us
  transfers between devices with their start and end apart: 41, of which 14 were waited for; matrix products, arithmetic and copies ran while one was open for 17% of the time, Pallas kernels for 30%

commit v1 on v0

--- a/solution.py
+++ b/solution.py
@@ -36,9 +36,9 @@
     half_width = head_width // 2
     freq_index = jnp.arange(half_width, dtype=jnp.float32)
     inv_freq = jnp.exp(freq_index * (-2.0 * math.log(theta_base) / head_width))
-    angles = position.astype(jnp.float32)[:, None] * inv_freq[None, :]
+    angles = inv_freq[:, None] * position.astype(jnp.float32)[None, :]
     cosine, sine = jnp.cos(angles), jnp.sin(angles)
-    return (jnp.concatenate([cosine, cosine], axis=1), jnp.concatenate([-sine, sine], axis=1))
+    return jnp.concatenate([cosine, cosine, -sine, sine], axis=0)
 
 
 def normalize(vector):
@@ -89,14 +89,15 @@
     return pl.BlockSpec(shape, lambda *_: (0,) * len(shape))
 
 
-def project_heads(h_one, weight, cos_tab, sin_tab, heads):
+def project_heads(h_one, weight, tables, heads):
     tok_count, width = h_one.shape
     cols = heads * HD
     rows = 2 * TILE
 
-    def body(h_ref, w_ref, c_ref, s_ref, q_ref, k_ref, v_ref):
+    def body(h_ref, w_ref, t_ref, q_ref, k_ref, v_ref):
         full = nn_dot(h_ref[...], w_ref[...])
-        cosine, sine = c_ref[...], s_ref[...]
+        turn = jnp.transpose(t_ref[...])
+        cosine, sine = turn[:, :HD], turn[:, HD:]
         for h in range(heads):
             u = full[:, h * HD : (h + 1) * HD]
             turned = (u * cosine + swap_halves(u) * sine).astype(jnp.bfloat16)
@@ -112,13 +113,12 @@
         in_specs=[
             pl.BlockSpec((rows, width), lambda i: (i, 0)),
             whole(weight.shape),
-            pl.BlockSpec((rows, HD), lambda i: (i, 0)),
-            pl.BlockSpec((rows, HD), lambda i: (i, 0)),
+            pl.BlockSpec((2 * HD, rows), lambda i: (0, i)),
         ],
         out_specs=[pl.BlockSpec((heads, rows, HD), lambda i: (0, i, 0))] * 3,
         out_shape=[out] * 3,
         name="project_heads",
-    )(h_one, weight, cos_tab, sin_tab)
+    )(h_one, weight, tables)
 
 
 def attend(first, last, place, query, key, value, seg_col, seg_row, parts):
@@ -209,7 +209,7 @@
 
 
 def attend_grad(
-    first, last, place, query, key, value, seg_col, seg_row, grads, out, lse, cos_tab, sin_tab
+    first, last, place, query, key, value, seg_col, seg_row, grads, out, lse, tables
 ):
     heads, tok_count, _ = query.shape
     blocks = tok_count // TILE
@@ -220,7 +220,7 @@
 
     def body(
         first_ref, last_ref, place_ref, q_ref, k_ref, v_ref, col_ref, row_ref, o_ref, lse_ref,
-        c_ref, s_ref, *refs
+        t_ref, *refs
     ):
         g_refs, (d_ref, split, inner, dq, dk, dv) = refs[:parts], refs[parts:]
         j = pl.program_id(0)
@@ -259,7 +259,8 @@
             return carry
 
         lax.fori_loop(lo, hi, step, 0)
-        cosine, sine = c_ref[here, :], s_ref[here, :]
+        turn = jnp.transpose(t_ref[:, here])
+        cosine, sine = turn[:, :HD], turn[:, HD:]
         for h in range(heads):
             w = dk[h]
             w = (w * cosine - swap_halves(w) * sine).astype(jnp.bfloat16)
@@ -270,9 +271,11 @@
         def _():
             for b in range(blocks):
                 rows = slice(b * TILE, (b + 1) * TILE)
+                turn = jnp.transpose(t_ref[:, rows])
+                cosine, sine = turn[:, :HD], turn[:, HD:]
                 for h in range(heads):
                     w = dq[h, rows, :] * HD**-0.5
-                    w = w * c_ref[rows, :] - swap_halves(w) * s_ref[rows, :]
+                    w = w * cosine - swap_halves(w) * sine
                     d_ref[rows, h * HD : (h + 1) * HD] = w.astype(jnp.bfloat16)
 
     return pl.pallas_call(
@@ -288,8 +291,7 @@
                 whole(seg_row.shape),
                 whole(out.shape),
                 whole(lse.shape),
-                whole(cos_tab.shape),
-                whole(sin_tab.shape),
+                whole(tables.shape),
             ]
             + [whole(g.shape) for g in grads],
             out_specs=whole((tok_count, 3 * cols)),
@@ -303,7 +305,7 @@
         ),
         out_shape=jax.ShapeDtypeStruct((tok_count, 3 * cols), jnp.bfloat16),
         name="attend_grad",
-    )(first, last, place, query, key, value, seg_col, seg_row, out, lse, cos_tab, sin_tab, *grads)
+    )(first, last, place, query, key, value, seg_col, seg_row, out, lse, tables, *grads)
 
 
 def swap(value, axis, step):
@@ -324,7 +326,7 @@
     lead, (rows, cols) = pieces[0].shape[:-2], pieces[0].shape[-2:]
     if rows % 16:
         order = place[0] ^ jnp.arange(count, dtype=jnp.int32)
-        ranked = jnp.take(jnp.stack(pieces), order, axis=0)
+        ranked = jnp.take(jnp.stack(pieces), order, axis=0, mode="clip")
         return jnp.moveaxis(ranked, 0, -3).reshape(*lead, count * rows, cols)
 
     kind = kind or pieces[0].dtype
@@ -351,7 +353,7 @@
     count = lax.axis_size("dp")
     rows, cols = total.shape[0] // count, total.shape[1]
     order = place[0] ^ jnp.array([*range(0, count, 2), *range(1, count, 2)], jnp.int32)
-    ranked = jnp.take(total.reshape(count, rows, cols), order, axis=0)
+    ranked = jnp.take(total.reshape(count, rows, cols), order, axis=0, mode="clip")
     return ranked[: count // 2], swap(ranked[count // 2 :], "dp", 1)
 
 
@@ -477,14 +479,19 @@
     here = slice(2 * side * hid, (2 * side + 2) * hid)
 
     def body(h_ref, f_ref, s_ref, c_ref, u_ref, l_ref, a_ref, b_ref, g_ref, out_ref):
-        for ref, turned, at in ((f_ref, h_ref, 0), (s_ref, h_ref, hid), (u_ref, c_ref, 2 * hid)):
-            full = tn_dot(turned[...], ref[:, here]).astype(jnp.bfloat16)
-            out_ref[0, :, at : at + hid] = full[:, :hid]
-            out_ref[1, :, at : at + hid] = full[:, hid:]
+        sides = jnp.concatenate([f_ref[:, here], s_ref[:, here]], axis=1)
+        full = tn_dot(h_ref[...], sides).astype(jnp.bfloat16)
+        for s in range(2):
+            out_ref[s, :, :hid] = full[:, s * hid : (s + 1) * hid]
+            out_ref[s, :, hid : 2 * hid] = full[:, (2 + s) * hid : (3 + s) * hid]
+        full = tn_dot(c_ref[...], u_ref[:, here]).astype(jnp.bfloat16)
+        heads = tn_dot(l_ref[...], jnp.concatenate([a_ref[...], b_ref[...]], axis=1))
+        heads = heads.astype(jnp.bfloat16)
         gain_col = jnp.transpose(jnp.broadcast_to(g_ref[...], (128, width))).astype(jnp.bfloat16)
-        for s, ref in ((0, a_ref), (1, b_ref)):
-            at = 3 * hid
-            out_ref[s, :, at : at + head_cols] = tn_dot(l_ref[...], ref[...]).astype(jnp.bfloat16)
+        at = 3 * hid
+        for s in range(2):
+            out_ref[s, :, 2 * hid : at] = full[:, s * hid : (s + 1) * hid]
+            out_ref[s, :, at : at + head_cols] = heads[:, s * head_cols : (s + 1) * head_cols]
             out_ref[s, :, at + head_cols :] = gain_col[:, : wide - at - head_cols]
 
     return pl.pallas_call(
@@ -519,8 +526,9 @@
 
 def share_rows(mine, place, kind=None):
     other = swap(mine, "tensor", 2)
-    far = swap(jnp.stack([mine, other]), "tensor", 1)
-    return assemble([mine, far[0], other, far[1]], place, kind)
+    beside = swap(mine, "tensor", 1)
+    across = swap(other, "tensor", 1)
+    return assemble([mine, beside, other, across], place, kind)
 
 
 def layer_shards(
@@ -559,18 +567,17 @@
     paired_far = gather_far(paired)
 
     segment, position = row_layout(lengths[0], tok_count)
-    cosine, sine_table = rotary_tables(position, HD)
+    tables = rotary_tables(position, HD)
     h_one = (normalize(tokens.astype(jnp.float32))[0] * attn_gain).astype(jnp.bfloat16)
     seg_col = jnp.broadcast_to(segment[:, None], (tok_count, TILE // 2))
     seg_row = segment[None, :]
     first, last = tile_ranges(lengths[0], tok_count)
-    query, key, value = project_heads(h_one, qkv_flat, cosine, sine_table, heads_dev)
+    query, key, value = project_heads(h_one, qkv_flat, tables, heads_dev)
     paired_far, query = lax.optimization_barrier((paired_far, query))
     pieces = gather_near(paired_far)
     *sent, attended_wide, log_total = attend(
         first, last, place, query, key, value, seg_col, seg_row, parts
     )
-    sent, pieces = lax.optimization_barrier((sent, pieces))
     weight_near = assemble(pieces, dp_place)
     weight_far = swap(weight_near, "tensor", 1)
     att = [sent[0]] + [swap(sent[r], "tensor", r) for r in range(1, parts)]
@@ -585,8 +592,9 @@
     grads_in = (h_two, d_first, d_second, my_cot, hidden, d_low, att, gain_two, wide)
     grads_far = weight_grads(1, *grads_in)
     grads_near = weight_grads(0, *grads_in)
-    chip = grads_near.astype(jnp.float32) + swap(grads_far, "tensor", 1).astype(jnp.float32)
-    chip_sent, d_att = lax.optimization_barrier((chip[1].astype(jnp.bfloat16), d_att))
+    grads_come = swap(grads_far, "tensor", 1)
+    chip_sent = grads_near[1].astype(jnp.float32) + grads_come[1].astype(jnp.float32)
+    chip_sent, d_att = lax.optimization_barrier((chip_sent.astype(jnp.bfloat16), d_att))
     column_come = swap(chip_sent, "tensor", 2)
 
     d_qkv = attend_grad(
@@ -601,27 +609,26 @@
         d_att,
         attended_wide,
         log_total,
-        cosine,
-        sine_table,
+        tables,
     )
     d_far = back_to_width(d_qkv, qkv_flat, place, (1, 3), share)
     d_near = back_to_width(d_qkv, qkv_flat, place, (0, 2), share)
-    d_chip = d_near.astype(jnp.float32) + swap(d_far, "tensor", 1).astype(jnp.float32)
+    d_side = swap(d_far, "tensor", 1)
+    d_sent = d_near[1].astype(jnp.float32) + d_side[1].astype(jnp.float32)
     d_sent, d_qkv, column_come = lax.optimization_barrier(
-        (d_chip[1].astype(jnp.bfloat16), d_qkv, column_come)
+        (d_sent.astype(jnp.bfloat16), d_qkv, column_come)
     )
     d_come = swap(d_sent, "tensor", 2)
-    column = (chip[0] + column_come.astype(jnp.float32)).astype(jnp.bfloat16)
+    column = grads_near[0].astype(jnp.float32) + grads_come[0].astype(jnp.float32)
+    column = (column + column_come.astype(jnp.float32)).astype(jnp.bfloat16)
     column_near, column_come = reduce_near(column, dp_place)
     qkv_total = jnp.einsum("td,tf->df", h_one, d_qkv, preferred_element_type=jnp.float32)
     qkv_near, qkv_come = reduce_near(qkv_total.astype(jnp.bfloat16), dp_place)
     normed_one, factor_one = normalize(my_tokens.astype(jnp.float32))
-    d_h_one = d_chip[0] + d_come.astype(jnp.float32)
+    d_h_one = d_near[0].astype(jnp.float32) + d_side[0].astype(jnp.float32)
+    d_h_one = d_h_one + d_come.astype(jnp.float32)
     tokens_grad = d_mid + norm_back(d_h_one, normed_one, factor_one, attn_gain)
-    tokens_grad, column_come, qkv_come = lax.optimization_barrier(
-        (tokens_grad.astype(jnp.bfloat16), column_come, qkv_come)
-    )
-    tokens_grad = share_rows(tokens_grad, place, jnp.float32)
+    tokens_grad = share_rows(tokens_grad.astype(jnp.bfloat16), place, jnp.float32)
     reduced = reduce_far(column_near, column_come)
     up_grad = reduced[:, : 2 * hid].reshape(rows, 2, hid)
     down_grad = reduced[:, 2 * hid : 3 * hid].T

time: 390 us -> 411 us (1.054)
  waiting for transfers between devices: 94.4 us -> 143 us
  local copies, waits for them, and re-layouts: 36.7 us -> 24.8 us
  other arithmetic: 42.7 us -> 31.3 us
  starting transfers between devices: 53.3 us -> 45.6 us
    ppermute x41 -> x43, waiting for transfers between devices: 94.4 us -> 143 us  [swap(): return lax.ppermute(value, axis, [(i, i ^ step) for i in range(count)])]
    ppermute x41 -> x43, starting transfers between devices: 53.3 us -> 45.6 us  [swap(): return lax.ppermute(value, axis, [(i, i ^ step) for i in range(count)])]
    add x2 -> x0, other arithmetic: 5.98 us -> none  [the longest x1 3.77 us: layer_shards(): grads_near.astype(jnp.float32)]
    squeeze x2 -> x0, local copies, waits for them, and re-layouts: 5.27 us -> none  [share_rows(): return assemble([mine, far[0], other, far[1]], place, kind)]
    convert_element_type x2 -> x4, other arithmetic: 4.08 us -> 9.31 us  [the longest x1 3.67 us: layer_shards(): chip_sent.astype(jnp.bfloat16)]
    unnamed x72 -> x58, local copies, waits for them, and re-layouts: 9.41 us -> 6.29 us
  transfers between devices with their start and end apart: 41 -> 43, of which waited for: 14 -> 17; matrix products, arithmetic and copies ran while one was open for 17% -> 14% of each run, Pallas kernels for 30% -> 14%
where the time goes in v1:
time: 411 us; the launch traced here: 403 us
  Pallas kernels  152 us (37%)
  waiting for transfers between devices  143 us (35%)
  starting transfers between devices  45.6 us (11%)
  other arithmetic  31.3 us (8%)
  local copies, waits for them, and re-layouts  24.8 us (6%)
  matrix products  4.85 us (1%)
    ppermute x43, waiting for transfers between devices, swap(): return lax.ppermute(value, axis, [(i, i ^ step) for i in range(count)])  143 us
    pallas_call x1, Pallas kernels, attend_grad(): pl.pallas_call(body, grid_spec=pltpu.PrefetchScalarGridSpec(num_scalar_pr...  56.7 us
    ppermute x43, starting transfers between devices, swap(): return lax.ppermute(value, axis, [(i, i ^ step) for i in range(count)])  45.6 us
    pallas_call x1, Pallas kernels, attend(): pl.pallas_call(body, grid_spec=pltpu.PrefetchScalarGridSpec(num_scalar_pr...  28.8 us
    pallas_call x1, Pallas kernels, layer(): pl.pallas_call(body, grid=(tok_count // rows,), in_specs=[tile(head_cols)...  19.7 us
    pallas_call x2, Pallas kernels, weight_grads(): pl.pallas_call(body, out_shape=jax.ShapeDtypeStruct((2, width, wide), jnp...  15.5 us
    pallas_call x4, Pallas kernels, assemble(): pl.pallas_call(body, grid_spec=pltpu.PrefetchScalarGridSpec(num_scalar_pr...  15.1 us
    pallas_call x1, Pallas kernels, project_heads(): pl.pallas_call(body, grid=(tok_count // rows,), in_specs=[pl.BlockSpec((r...  8.22 us
  transfers between devices with their start and end apart: 43, of which 17 were waited for; matrix products, arithmetic and copies ran while one was open for 14% of the time, Pallas kernels for 14%

profile of v1, /device:TPU:0, one launch (start us, length us, event | category | flops | bytes accessed | tf_op | source)
XLA Modules:
  0.0 403.3 jit_solution(10751334201028992729)
XLA Ops:
  2.0 5.1 %collective-permute-start.3 = (bf16[96,576]{1,0:T(8,128)(2,1)S(1)}, bf16[96,576]{1,0:T(8,128)(2,1)}, u32[]{:S(2)}, u32[]{:S(2)}) collective-permute-start(bf16[96,576]{1,0:T(8,128)(2,1)S(1)} %copy.58.refs_0_), channel_id=1, source_target_pairs={{0,24},{4,28},{8,16},{12,20},{16,8},{20,12},{24,0},{28,4},{1,25},{... | collective-permute-start | bytes 331784 | tf_op jit(solution)/shard_map/ppermute | solution.py:313
  17.9 2.5 convert_reduce_fusion
  27.8 2.9 collective-permute-start.5
  41.6 8.2 %project_heads.1 = (bf16[3,2048,64]{2,1,0:T(8,128)(2,1)}, bf16[3,2048,64]{2,1,0:T(8,128)(2,1)}, bf16[3,2048,64]{2,1,0:T(8,128)(2,1)}) custom-call(bf16[2048,768]{1,0:T(8,128)(2,1)} %fusion.4.h_ref, bf16[768,576]{1,0:T(8,128)(2,1)} %assemble.4.w_ref, f32[128,2048]{1,0:T(8,128)} %pad_maximum_fusion.t_ref), custom_call_target="tpu_custom_call" | custom-call | tf_op jit(solution)/shard_map/project_heads/pallas_call | solution.py:110
  49.8 11.2 %collective-permute-done.5.refs_4_ = bf16[2,96,1152]{2,1,0:T(8,128)(2,1)} collective-permute-done((bf16[2,96,1152]{2,1,0:T(8,128)(2,1)}, bf16[2,96,1152]{2,1,0:T(8,128)(2,1)}, u32[]{:S(2)}, u32[]{:S(2)}) %collective-permute-start.5) | collective-permute-done | bytes 442400 | tf_op jit(solution)/shard_map/ppermute | solution.py:313
  65.1 9.3 %collective-permute-done.14.refs_1_ = bf16[2,96,1152]{2,1,0:T(8,128)(2,1)} collective-permute-done((bf16[2,96,1152]{2,1,0:T(8,128)(2,1)}, bf16[2,96,1152]{2,1,0:T(8,128)(2,1)}, u32[]{:S(2)}, u32[]{:S(2)}) %collective-permute-start.14) | collective-permute-done | bytes 442400 | tf_op jit(solution)/shard_map/ppermute | solution.py:313
  74.4 9.5 %collective-permute-done.15.refs_3_ = bf16[2,96,1152]{2,1,0:T(8,128)(2,1)} collective-permute-done((bf16[2,96,1152]{2,1,0:T(8,128)(2,1)}, bf16[2,96,1152]{2,1,0:T(8,128)(2,1)}, u32[]{:S(2)}, u32[]{:S(2)}) %collective-permute-start.15) | collective-permute-done | bytes 442400 | tf_op jit(solution)/shard_map/ppermute | solution.py:313
  83.9 7.7 %collective-permute-done.16.refs_5_ = bf16[2,96,1152]{2,1,0:T(8,128)(2,1)} collective-permute-done((bf16[2,96,1152]{2,1,0:T(8,128)(2,1)}, bf16[2,96,1152]{2,1,0:T(8,128)(2,1)}, u32[]{:S(2)}, u32[]{:S(2)}) %collective-permute-start.16) | collective-permute-done | bytes 442400 | tf_op jit(solution)/shard_map/ppermute | solution.py:313
  91.6 4.7 %collective-permute-done.17.refs_7_ = bf16[2,96,1152]{2,1,0:T(8,128)(2,1)} collective-permute-done((bf16[2,96,1152]{2,1,0:T(8,128)(2,1)}, bf16[2,96,1152]{2,1,0:T(8,128)(2,1)}, u32[]{:S(2)}, u32[]{:S(2)}) %collective-permute-start.17) | collective-permute-done | bytes 442400 | tf_op jit(solution)/shard_map/ppermute | solution.py:313
  96.3 4.0 assemble.5.refs_7_
  102.4 28.8 %attend.1 = (bf16[512,192]{1,0:T(8,128)(2,1)}, bf16[512,192]{1,0:T(8,128)(2,1)}, bf16[512,192]{1,0:T(8,128)(2,1)}, bf16[512,192]{1,0:T(8,128)(2,1)}, f32[3,2048,64]{2,1,0:T(8,128)}, /*index=5*/f32[3,1,2048]{2,1,0:T(1,128)}) custom-call(s32[8]{0:T(128)} %get-tuple-element.142.first_ref, s32[8]{0:T(128)} %get-tuple-element.141.last_ref, s32[1]{0:T(128)} %bitcast.place_ref, ...), custom_call_target="tpu_custom_call" | custom-call | tf_op jit(solution)/shard_map/attend/pallas_call | solution.py:177
  136.9 4.3 %collective-permute-done.12.refs_2_.b_ref = bf16[512,192]{1,0:T(8,128)(2,1)S(1)} collective-permute-done((bf16[512,192]{1,0:T(8,128)(2,1)}, bf16[512,192]{1,0:T(8,128)(2,1)S(1)}, u32[]{:S(2)}, u32[]{:S(2)}) %collective-permute-start.12) | collective-permute-done | bytes 196640 | tf_op jit(solution)/shard_map/ppermute | solution.py:313
  141.2 3.8 collective-permute-done.13.refs_3_.b_ref
  145.7 19.7 %layer.1 = (bf16[512,768]{1,0:T(8,128)(2,1)}, f32[512,768]{1,0:T(8,128)}, bf16[512,768]{1,0:T(8,128)(2,1)}, bf16[512,768]{1,0:T(8,128)(2,1)}, bf16[512,1152]{1,0...) custom-call(bf16[512,192]{1,0:T(8,128)(2,1)} %get-tuple-element.56.r, ...), custom_call_target="tpu_custom_call" | custom-call | tf_op jit(solution)/shard_map/layer/pallas_call | solution.py:440
  165.4 8.0 %weight_grads.3 = bf16[2,768,1152]{2,1,0:T(8,128)(2,1)} custom-call(bf16[512,768]{1,0:T(8,128)(2,1)} %get-tuple-element.68.h_ref, bf16[512,1152]{1,0:T(8,128)(2,1)} %get-tuple-element.69.f_ref, bf16[512,1152]{1,0:T(8,128)(2,1)} %get-tuple-element.70.s_ref, bf16[512,768]{1,0:T(8,128)(2,1)} %constant_dynamic-slice_fusion.refs_5_.c_ref, ...), custom_call_target="tpu_custom_call" | custom-call | tf_op jit(solution)/shard_map/weight_grads/pallas_call | solution.py:497
  176.0 7.4 %weight_grads.2 = bf16[2,768,1152]{2,1,0:T(8,128)(2,1)} custom-call(bf16[512,768]{1,0:T(8,128)(2,1)} %get-tuple-element.68.h_ref, bf16[512,1152]{1,0:T(8,128)(2,1)} %get-tuple-element.69.f_ref, bf16[512,1152]{1,0:T(8,128)(2,1)} %get-tuple-element.70.s_ref, bf16[512,768]{1,0:T(8,128)(2,1)} %constant_dynamic-slice_fusion.refs_5_.c_ref, ...), custom_call_target="tpu_custom_call" | custom-call | tf_op jit(solution)/shard_map/weight_grads/pallas_call | solution.py:497
  183.5 3.7 fusion.10
  188.7 56.7 %attend_grad.1.d_ref = bf16[2048,576]{1,0:T(8,128)(2,1)} custom-call(s32[8]{0:T(128)} %get-tuple-element.142.first_ref, s32[8]{0:T(128)} %get-tuple-element.141.last_ref, s32[1]{0:T(128)} %bitcast.place_ref, bf16[3,2048,64]{2,1,0:T(8,128)(2,1)} %get-tuple-element.53.q_ref, bf16[3,2048,64]{2,1,0:T(8,128)(2,1)} %get-tuple-element.54.k_ref, ...), custom_call_target="tpu_custom_call" | custom-call | tf_op jit(solution)/shard_map/attend_grad/pallas_call | solution.py:281
  245.4 4.0 back_to_width.3
  251.9 55.7 %collective-permute-done.20.refs_2_ = bf16[512,768]{1,0:T(8,128)(2,1)} collective-permute-done((bf16[512,768]{1,0:T(8,128)(2,1)}, bf16[512,768]{1,0:T(8,128)(2,1)}, u32[]{:S(2)}, u32[]{:S(2)}) %collective-permute-start.20) | collective-permute-done | bytes 786464 | tf_op jit(solution)/shard_map/ppermute | solution.py:313
  307.6 4.1 %back_to_width.2 = bf16[2,512,768]{2,1,0:T(8,128)(2,1)} custom-call(s32[1]{0:T(128)} %bitcast.place_ref, bf16[2048,576]{1,0:T(8,128)(2,1)} %attend_grad.1.d_ref, bf16[768,576]{1,0:T(8,128)(2,1)} %assemble.4.w_ref), custom_call_target="tpu_custom_call" | custom-call | tf_op jit(solution)/shard_map/back_to_width/pallas_call | solution.py:511
  311.7 2.5 fusion.18
  314.2 4.8 %convolution_convert_fusion = bf16[768,576]{0,1:T(8,128)(2,1)} fusion(bf16[2048,768]{1,0:T(8,128)(2,1)} %fusion.4.h_ref, bf16[2048,576]{1,0:T(8,128)(2,1)S(1)} %copy-done.3), kind=kOutput, calls=%fused_computation.29 | convolution fusion | flops 1812381696 | bytes 6389760 | tf_op jit(solution)/shard_map/td,tf->df/dot_general | solution.py:625
  322.3 3.7 assemble.6
  326.6 8.7 %collective-permute-done.32 = bf16[4,96,576]{2,1,0:T(8,128)(2,1)S(1)} collective-permute-done((bf16[4,96,576]{2,1,0:T(8,128)(2,1)S(1)}, bf16[4,96,576]{2,1,0:T(8,128)(2,1)S(1)}, u32[]{:S(2)}, u32[]{:S(2)}) %collective-permute-start.32) | collective-permute-done | bytes 442400 | tf_op jit(solution)/shard_map/ppermute | solution.py:313
  336.4 6.9 %collective-permute-start.33 = (bf16[96,576]{1,0:T(8,128)(2,1)S(1)}, bf16[96,576]{1,0:T(8,128)(2,1)S(1)}, u32[]{:S(2)}, u32[]{:S(2)}) collective-permute-start(bf16[96,576]{1,0:T(8,128)(2,1)S(1)} %get-tuple-element.135), channel_id=1, source_target_pairs={{0,8},{4,12},{8,0},{12,4},{16,24},{20,28},{24,16},{28,20},{1,9},{5... | collective-permute-start | bytes 331784 | tf_op jit(solution)/shard_map/ppermute | solution.py:313
  345.7 3.2 fusion.5
  350.9 2.3 slice.115
  364.8 9.5 %collective-permute-done.39 = bf16[4,96,1152]{2,1,0:T(8,128)(2,1)} collective-permute-done((bf16[4,96,1152]{2,1,0:T(8,128)(2,1)}, bf16[4,96,1152]{2,1,0:T(8,128)(2,1)}, u32[]{:S(2)}, u32[]{:S(2)}) %collective-permute-start.39) | collective-permute-done | bytes 884768 | tf_op jit(solution)/shard_map/ppermute | solution.py:313
  380.8 3.4 collective-permute-done.30.refs_2_
  385.5 8.9 %collective-permute-done.41 = bf16[96,1152]{1,0:T(8,128)(2,1)S(1)} collective-permute-done((bf16[96,1152]{1,0:T(8,128)(2,1)S(1)}, bf16[96,1152]{1,0:T(8,128)(2,1)S(1)}, u32[]{:S(2)}, u32[]{:S(2)}) %collective-permute-start.41) | collective-permute-done | bytes 221216 | tf_op jit(solution)/shard_map/ppermute | solution.py:313
  397.9 5.1 %assemble.7 = f32[2048,768]{1,0:T(8,128)} custom-call(s32[1]{0:T(128)} %bitcast.place_ref, bf16[512,768]{1,0:T(8,128)(2,1)} %copy-done.7, bf16[512,768]{1,0:T(8,128)(2,1)} %collective-permute-done.29.refs_1_, bf16[512,768]{1,0:T(8,128)(2,1)} %collective-permute-done.30.refs_2_, bf16[512,768]{1,0:T(8,128)(2,1)} %collective-permute-done.31.refs_3_), custom_call_target="tpu_custom_call" | custom-call | tf_op jit(solution)/shard_map/assemble/pallas_call | solution.py:339
  (184 shorter events, 81.4 us)
Async XLA Ops:
  2.0 22.2 %collective-permute-start.3 = (bf16[96,576]{1,0:T(8,128)(2,1)S(1)}, bf16[96,576]{1,0:T(8,128)(2,1)}, u32[]{:S(2)}, u32[]{:S(2)}) collective-permute-start(bf16[96,576]{1,0:T(8,128)(2,1)S(1)} %copy.58.refs_0_), channel_id=1, source_target_pairs={{0,24},{4,28},{8,16},{12,20},{16,8},{20,12},{24,0},{28,4},{1,25},{... | collective-permute-start | bytes 331784 | tf_op jit(solution)/shard_map/ppermute | solution.py:313
  7.2 19.3 %collective-permute-start.1 = (bf16[96,576]{1,0:T(8,128)(2,1)S(1)}, bf16[96,576]{1,0:T(8,128)(2,1)}, u32[]{:S(2)}, u32[]{:S(2)}) collective-permute-start(bf16[96,576]{1,0:T(8,128)(2,1)S(1)} %copy.58.refs_0_), channel_id=1, source_target_pairs={{0,8},{4,12},{8,0},{12,4},{16,24},{20,28},{24,16},{28,20},{1,9},{5... | collective-permute-start | bytes 331784 | tf_op jit(solution)/shard_map/ppermute | solution.py:313
  7.2 19.3 %collective-permute-start.2 = (bf16[96,576]{1,0:T(8,128)(2,1)S(1)}, bf16[96,576]{1,0:T(8,128)(2,1)}, u32[]{:S(2)}, u32[]{:S(2)}) collective-permute-start(bf16[96,576]{1,0:T(8,128)(2,1)S(1)} %copy.58.refs_0_), channel_id=1, source_target_pairs={{0,16},{4,20},{8,24},{12,28},{16,0},{20,4},{24,8},{28,12},{1,17},{... | collective-permute-start | bytes 331784 | tf_op jit(solution)/shard_map/ppermute | solution.py:313
  7.8 24.1 %collective-permute-start.7 = (bf16[96,576]{1,0:T(8,128)(2,1)S(1)}, bf16[96,576]{1,0:T(8,128)(2,1)}, u32[]{:S(2)}, u32[]{:S(2)}) collective-permute-start(bf16[96,576]{1,0:T(8,128)(2,1)S(1)} %copy.58.refs_0_), channel_id=1, source_target_pairs={{0,4},{4,0},{8,12},{12,8},{16,20},{20,16},{24,28},{28,24},{1,5},{5... | collective-permute-start | bytes 331784 | tf_op jit(solution)/shard_map/ppermute | solution.py:313
  26.5 23.3 %collective-permute-start.4 = (bf16[2,96,1152]{2,1,0:T(8,128)(2,1)}, bf16[2,96,1152]{2,1,0:T(8,128)(2,1)}, u32[]{:S(2)}, u32[]{:S(2)}) collective-permute-start(bf16[2,96,1152]{2,1,0:T(8,128)(2,1)} %pad_maximum_fusion.1.refs_0_), channel_id=1, source_target_pairs={{0,8},{4,12},{8,0},{12,4},{16,24},{20,28},{24,16},{28,20},{1,9},{5... | collective-permute-start | bytes 1327112 | tf_op jit(solution)/shard_map/ppermute | solution.py:313
  27.8 33.2 %collective-permute-start.5 = (bf16[2,96,1152]{2,1,0:T(8,128)(2,1)}, bf16[2,96,1152]{2,1,0:T(8,128)(2,1)}, u32[]{:S(2)}, u32[]{:S(2)}) collective-permute-start(bf16[2,96,1152]{2,1,0:T(8,128)(2,1)} %pad_maximum_fusion.1.refs_0_), channel_id=1, source_target_pairs={{0,16},{4,20},{8,24},{12,28},{16,0},{20,4},{24,8},{28,12},{1,17},{... | collective-permute-start | bytes 1327112 | tf_op jit(solution)/shard_map/ppermute | solution.py:313
  30.7 30.3 %collective-permute-start.6 = (bf16[2,96,1152]{2,1,0:T(8,128)(2,1)}, bf16[2,96,1152]{2,1,0:T(8,128)(2,1)}, u32[]{:S(2)}, u32[]{:S(2)}) collective-permute-start(bf16[2,96,1152]{2,1,0:T(8,128)(2,1)} %pad_maximum_fusion.1.refs_0_), channel_id=1, source_target_pairs={{0,24},{4,28},{8,16},{12,20},{16,8},{20,12},{24,0},{28,4},{1,25},{... | collective-permute-start | bytes 1327112 | tf_op jit(solution)/shard_map/ppermute | solution.py:313
  61.0 13.4 %collective-permute-start.14 = (bf16[2,96,1152]{2,1,0:T(8,128)(2,1)}, bf16[2,96,1152]{2,1,0:T(8,128)(2,1)}, u32[]{:S(2)}, u32[]{:S(2)}) collective-permute-start(bf16[2,96,1152]{2,1,0:T(8,128)(2,1)} %pad_maximum_fusion.1.refs_0_), channel_id=1, source_target_pairs={{0,4},{4,0},{8,12},{12,8},{16,20},{20,16},{24,28},{28,24},{1,5},{5... | collective-permute-start | bytes 1327112 | tf_op jit(solution)/shard_map/ppermute | solution.py:313
  62.5 21.3 %collective-permute-start.15 = (bf16[2,96,1152]{2,1,0:T(8,128)(2,1)}, bf16[2,96,1152]{2,1,0:T(8,128)(2,1)}, u32[]{:S(2)}, u32[]{:S(2)}) collective-permute-start(bf16[2,96,1152]{2,1,0:T(8,128)(2,1)} %collective-permute-done.4.refs_2_), channel_id=1, source_target_pairs={{0,4},{4,0},{8,12},{12,8},{16,20},{20,16},{24,28},{28,24},{1,5},{5... | collective-permute-start | bytes 1327112 | tf_op jit(solution)/shard_map/ppermute | solution.py:313
  63.1 28.5 %collective-permute-start.16 = (bf16[2,96,1152]{2,1,0:T(8,128)(2,1)}, bf16[2,96,1152]{2,1,0:T(8,128)(2,1)}, u32[]{:S(2)}, u32[]{:S(2)}) collective-permute-start(bf16[2,96,1152]{2,1,0:T(8,128)(2,1)} %collective-permute-done.5.refs_4_), channel_id=1, source_target_pairs={{0,4},{4,0},{8,12},{12,8},{16,20},{20,16},{24,28},{28,24},{1,5},{5... | collective-permute-start | bytes 1327112 | tf_op jit(solution)/shard_map/ppermute | solution.py:313
  64.6 31.8 %collective-permute-start.17 = (bf16[2,96,1152]{2,1,0:T(8,128)(2,1)}, bf16[2,96,1152]{2,1,0:T(8,128)(2,1)}, u32[]{:S(2)}, u32[]{:S(2)}) collective-permute-start(bf16[2,96,1152]{2,1,0:T(8,128)(2,1)} %collective-permute-done.6.refs_6_), channel_id=1, source_target_pairs={{0,4},{4,0},{8,12},{12,8},{16,20},{20,16},{24,28},{28,24},{1,5},{5... | collective-permute-start | bytes 1327112 | tf_op jit(solution)/shard_map/ppermute | solution.py:313
  100.3 45.4 %collective-permute-start.18 = (bf16[2,768,1152]{2,1,0:T(8,128)(2,1)}, bf16[2,768,1152]{2,1,0:T(8,128)(2,1)}, u32[]{:S(2)}, u32[]{:S(2)}) collective-permute-start(bf16[2,768,1152]{2,1,0:T(8,128)(2,1)} %assemble.5.refs_7_), channel_id=1, source_target_pairs={{0,1},{1,0},{2,3},{3,2},{4,5},{5,4},{6,7},{7,6},{8,9},{9,8},{10,11... | collective-permute-start | bytes 10616840 | tf_op jit(solution)/shard_map/ppermute | solution.py:313
  174.2 13.0 %collective-permute-start.23 = (bf16[512,192]{1,0:T(8,128)(2,1)S(1)}, bf16[512,192]{1,0:T(8,128)(2,1)S(1)}, u32[]{:S(2)}, u32[]{:S(2)}) collective-permute-start(bf16[512,192]{1,0:T(8,128)(2,1)S(1)} %copy-done.25), channel_id=1, source_target_pairs={{0,1},{1,0},{2,3},{3,2},{4,5},{5,4},{6,7},{7,6},{8,9},{9,8},{10,11... | collective-permute-start | bytes 589832 | tf_op jit(solution)/shard_map/ppermute | solution.py:313
  174.3 12.9 %collective-permute-start.24 = (bf16[512,192]{1,0:T(8,128)(2,1)S(1)}, bf16[512,192]{1,0:T(8,128)(2,1)S(1)}, u32[]{:S(2)}, u32[]{:S(2)}) collective-permute-start(bf16[512,192]{1,0:T(8,128)(2,1)S(1)} %copy-done.24), channel_id=1, source_target_pairs={{0,2},{1,3},{2,0},{3,1},{4,6},{5,7},{6,4},{7,5},{8,10},{9,11},{10,... | collective-permute-start | bytes 589832 | tf_op jit(solution)/shard_map/ppermute | solution.py:313
  174.8 13.2 %collective-permute-start.25 = (bf16[512,192]{1,0:T(8,128)(2,1)S(1)}, bf16[512,192]{1,0:T(8,128)(2,1)S(1)}, u32[]{:S(2)}, u32[]{:S(2)}) collective-permute-start(bf16[512,192]{1,0:T(8,128)(2,1)S(1)} %copy-done.23), channel_id=1, source_target_pairs={{0,3},{1,2},{2,1},{3,0},{4,7},{5,6},{6,5},{7,4},{8,11},{9,10},{10,... | collective-permute-start | bytes 589832 | tf_op jit(solution)/shard_map/ppermute | solution.py:313
  249.4 62.3 %collective-permute-start.26 = (bf16[2,512,768]{2,1,0:T(8,128)(2,1)}, bf16[2,512,768]{2,1,0:T(8,128)(2,1)}, u32[]{:S(2)}, u32[]{:S(2)}) collective-permute-start(bf16[2,512,768]{2,1,0:T(8,128)(2,1)} %back_to_width.3), channel_id=1, source_target_pairs={{0,1},{1,0},{2,3},{3,2},{4,5},{5,4},{6,7},{7,6},{8,9},{9,8},{10,11... | collective-permute-start | bytes 4718600 | tf_op jit(solution)/shard_map/ppermute | solution.py:313
  249.8 64.4 %collective-permute-start.27 = (bf16[768,1152]{1,0:T(8,128)(2,1)}, bf16[768,1152]{1,0:T(8,128)(2,1)}, u32[]{:S(2)}, u32[]{:S(2)}) collective-permute-start(bf16[768,1152]{1,0:T(8,128)(2,1)} %fusion.10), channel_id=1, source_target_pairs={{0,2},{1,3},{2,0},{3,1},{4,6},{5,7},{6,4},{7,5},{8,10},{9,11},{10,... | collective-permute-start | bytes 5308424 | tf_op jit(solution)/shard_map/ppermute | solution.py:313
  250.3 57.3 %collective-permute-start.20 = (bf16[512,768]{1,0:T(8,128)(2,1)}, bf16[512,768]{1,0:T(8,128)(2,1)}, u32[]{:S(2)}, u32[]{:S(2)}) collective-permute-start(bf16[512,768]{1,0:T(8,128)(2,1)} %get-tuple-element.64.refs_0_), channel_id=1, source_target_pairs={{0,2},{1,3},{2,0},{3,1},{4,6},{5,7},{6,4},{7,5},{8,10},{9,11},{10,... | collective-permute-start | bytes 2359304 | tf_op jit(solution)/shard_map/ppermute | solution.py:313
  251.8 70.5 %collective-permute-start.19 = (bf16[512,768]{1,0:T(8,128)(2,1)}, bf16[512,768]{1,0:T(8,128)(2,1)}, u32[]{:S(2)}, u32[]{:S(2)}) collective-permute-start(bf16[512,768]{1,0:T(8,128)(2,1)} %get-tuple-element.64.refs_0_), channel_id=1, source_target_pairs={{0,1},{1,0},{2,3},{3,2},{4,5},{5,4},{6,7},{7,6},{8,9},{9,8},{10,11... | collective-permute-start | bytes 2359304 | tf_op jit(solution)/shard_map/ppermute | solution.py:313
  307.6 14.7 %collective-permute-start.21 = (bf16[512,768]{1,0:T(8,128)(2,1)}, bf16[512,768]{1,0:T(8,128)(2,1)}, u32[]{:S(2)}, u32[]{:S(2)}) collective-permute-start(bf16[512,768]{1,0:T(8,128)(2,1)} %collective-permute-done.20.refs_2_), channel_id=1, source_target_pairs={{0,1},{1,0},{2,3},{3,2},{4,5},{5,4},{6,7},{7,6},{8,9},{9,8},{10,11... | collective-permute-start | bytes 2359304 | tf_op jit(solution)/shard_map/ppermute | solution.py:313
  321.6 13.7 %collective-permute-start.32 = (bf16[4,96,576]{2,1,0:T(8,128)(2,1)S(1)}, bf16[4,96,576]{2,1,0:T(8,128)(2,1)S(1)}, u32[]{:S(2)}, u32[]{:S(2)}) collective-permute-start(bf16[4,96,576]{2,1,0:T(8,128)(2,1)S(1)} %slice.107), channel_id=1, source_target_pairs={{0,4},{4,0},{8,12},{12,8},{16,20},{20,16},{24,28},{28,24},{1,5},{5... | collective-permute-start | bytes 1327112 | tf_op jit(solution)/shard_map/ppermute | solution.py:313
  326.0 33.6 %collective-permute-start.28 = (bf16[512,768]{1,0:T(8,128)(2,1)}, bf16[512,768]{1,0:T(8,128)(2,1)}, u32[]{:S(2)}, u32[]{:S(2)}) collective-permute-start(bf16[512,768]{1,0:T(8,128)(2,1)} %fusion.18), channel_id=1, source_target_pairs={{0,2},{1,3},{2,0},{3,1},{4,6},{5,7},{6,4},{7,5},{8,10},{9,11},{10,... | collective-permute-start | bytes 2359304 | tf_op jit(solution)/shard_map/ppermute | solution.py:313
  336.4 18.3 %collective-permute-start.33 = (bf16[96,576]{1,0:T(8,128)(2,1)S(1)}, bf16[96,576]{1,0:T(8,128)(2,1)S(1)}, u32[]{:S(2)}, u32[]{:S(2)}) collective-permute-start(bf16[96,576]{1,0:T(8,128)(2,1)S(1)} %get-tuple-element.135), channel_id=1, source_target_pairs={{0,8},{4,12},{8,0},{12,4},{16,24},{20,28},{24,16},{28,20},{1,9},{5... | collective-permute-start | bytes 331784 | tf_op jit(solution)/shard_map/ppermute | solution.py:313
  353.2 21.0 %collective-permute-start.39 = (bf16[4,96,1152]{2,1,0:T(8,128)(2,1)}, bf16[4,96,1152]{2,1,0:T(8,128)(2,1)}, u32[]{:S(2)}, u32[]{:S(2)}) collective-permute-start(bf16[4,96,1152]{2,1,0:T(8,128)(2,1)} %slice.115), channel_id=1, source_target_pairs={{0,4},{4,0},{8,12},{12,8},{16,20},{20,16},{24,28},{28,24},{1,5},{5... | collective-permute-start | bytes 2654216 | tf_op jit(solution)/shard_map/ppermute | solution.py:313
  356.6 19.9 %collective-permute-start.36 = (f32[96]{0:T(128)S(1)}, f32[96]{0:T(128)S(1)}, u32[]{:S(2)}, u32[]{:S(2)}) collective-permute-start(f32[96]{0:T(128)S(1)} %get-tuple-element.124), channel_id=1, source_target_pairs={{0,1},{1,0},{2,3},{3,2},{4,5},{5,4},{6,7},{7,6},{8,9},{9,8},{10,11... | collective-permute-start | bytes 1160 | tf_op jit(solution)/shard_map/ppermute | solution.py:313
  356.7 22.1 %collective-permute-start.37 = (f32[96]{0:T(128)S(1)}, f32[96]{0:T(128)S(1)}, u32[]{:S(2)}, u32[]{:S(2)}) collective-permute-start(f32[96]{0:T(128)S(1)} %get-tuple-element.124), channel_id=1, source_target_pairs={{0,2},{1,3},{2,0},{3,1},{4,6},{5,7},{6,4},{7,5},{8,10},{9,11},{10,... | collective-permute-start | bytes 1160 | tf_op jit(solution)/shard_map/ppermute | solution.py:313
  357.3 22.8 %collective-permute-start.38 = (f32[96]{0:T(128)S(1)}, f32[96]{0:T(128)S(1)}, u32[]{:S(2)}, u32[]{:S(2)}) collective-permute-start(f32[96]{0:T(128)S(1)} %get-tuple-element.124), channel_id=1, source_target_pairs={{0,3},{1,2},{2,1},{3,0},{4,7},{5,6},{6,5},{7,4},{8,11},{9,10},{10,... | collective-permute-start | bytes 1160 | tf_op jit(solution)/shard_map/ppermute | solution.py:313
  364.2 20.0 %collective-permute-start.30 = (bf16[512,768]{1,0:T(8,128)(2,1)S(1)}, bf16[512,768]{1,0:T(8,128)(2,1)}, u32[]{:S(2)}, u32[]{:S(2)}) collective-permute-start(bf16[512,768]{1,0:T(8,128)(2,1)S(1)} %fusion.15.refs_0_), channel_id=1, source_target_pairs={{0,2},{1,3},{2,0},{3,1},{4,6},{5,7},{6,4},{7,5},{8,10},{9,11},{10,... | collective-permute-start | bytes 2359304 | tf_op jit(solution)/shard_map/ppermute | solution.py:313
  376.5 17.9 %collective-permute-start.41 = (bf16[96,1152]{1,0:T(8,128)(2,1)S(1)}, bf16[96,1152]{1,0:T(8,128)(2,1)S(1)}, u32[]{:S(2)}, u32[]{:S(2)}) collective-permute-start(bf16[96,1152]{1,0:T(8,128)(2,1)S(1)} %get-tuple-element.134), channel_id=1, source_target_pairs={{0,16},{4,20},{8,24},{12,28},{16,0},{20,4},{24,8},{28,12},{1,17},{... | collective-permute-start | bytes 663560 | tf_op jit(solution)/shard_map/ppermute | solution.py:313
  378.8 15.7 %collective-permute-start.42 = (bf16[96,1152]{1,0:T(8,128)(2,1)S(1)}, bf16[96,1152]{1,0:T(8,128)(2,1)S(1)}, u32[]{:S(2)}, u32[]{:S(2)}) collective-permute-start(bf16[96,1152]{1,0:T(8,128)(2,1)S(1)} %get-tuple-element.133), channel_id=1, source_target_pairs={{0,24},{4,28},{8,16},{12,20},{16,8},{20,12},{24,0},{28,4},{1,25},{... | collective-permute-start | bytes 663560 | tf_op jit(solution)/shard_map/ppermute | solution.py:313
  380.8 17.2 %collective-permute-start.29 = (bf16[512,768]{1,0:T(8,128)(2,1)S(1)}, bf16[512,768]{1,0:T(8,128)(2,1)}, u32[]{:S(2)}, u32[]{:S(2)}) collective-permute-start(bf16[512,768]{1,0:T(8,128)(2,1)S(1)} %fusion.15.refs_0_), channel_id=1, source_target_pairs={{0,1},{1,0},{2,3},{3,2},{4,5},{5,4},{6,7},{7,6},{8,9},{9,8},{10,11... | collective-permute-start | bytes 2359304 | tf_op jit(solution)/shard_map/ppermute | solution.py:313
  384.2 13.8 %collective-permute-start.31 = (bf16[512,768]{1,0:T(8,128)(2,1)}, bf16[512,768]{1,0:T(8,128)(2,1)}, u32[]{:S(2)}, u32[]{:S(2)}) collective-permute-start(bf16[512,768]{1,0:T(8,128)(2,1)} %collective-permute-done.30.refs_2_), channel_id=1, source_target_pairs={{0,1},{1,0},{2,3},{3,2},{4,5},{5,4},{6,7},{7,6},{8,9},{9,8},{10,11... | collective-permute-start | bytes 2359304 | tf_op jit(solution)/shard_map/ppermute | solution.py:313
  (38 other events, 476.2 us)

commit v2 on v1

--- a/solution.py
+++ b/solution.py
@@ -159,13 +159,18 @@
             return carry
 
         lax.fori_loop(lo, hi, spread, 0)
+        lane = lax.broadcasted_iota(jnp.int32, (TILE, half), 1)
+        norms, peaks = jnp.ones((TILE, half), jnp.float32), peak[0]
         for h in range(heads):
             norm = jnp.sum(total[h], axis=1, keepdims=True)
+            norms = jnp.where(lane == h, norm, norms)
+            peaks = jnp.where(lane == h, peak[h], peaks)
             out = accum[h] / norm
             out_ref[h] = out
             low[:, h * HD : (h + 1) * HD] = out.astype(jnp.bfloat16)
-            logs = peak[h] + jnp.log(jnp.broadcast_to(norm, (TILE, half)))
-            lse_ref[h] = jnp.transpose(logs)[0:1, :]
+        logs = jnp.transpose(peaks + jnp.log(norms))
+        for h in range(heads):
+            lse_ref[h] = logs[h : h + 1, :]
         rows = pl.ds(pl.multiple_of((i % share) * TILE, TILE), TILE)
         for r in range(parts):
 
@@ -209,12 +214,13 @@
 
 
 def attend_grad(
-    first, last, place, query, key, value, seg_col, seg_row, grads, out, lse, tables
+    first, last, place, query, key, value, seg_col, seg_row, grads, out, lse, tables, head, done
 ):
-    heads, tok_count, _ = query.shape
+    all_heads, tok_count, _ = query.shape
+    heads = all_heads - 1 if head == 0 else 1
     blocks = tok_count // TILE
     half = TILE // 2
-    cols = heads * HD
+    cols = all_heads * HD
     parts = len(grads)
     share = tok_count // parts
 
@@ -222,7 +228,8 @@
         first_ref, last_ref, place_ref, q_ref, k_ref, v_ref, col_ref, row_ref, o_ref, lse_ref,
         t_ref, *refs
     ):
-        g_refs, (d_ref, split, inner, dq, dk, dv) = refs[:parts], refs[parts:]
+        g_refs, done_refs = refs[:parts], refs[parts:-6]
+        d_ref, split, inner, dq, dk, dv = refs[-6:]
         j = pl.program_id(0)
         lo, hi = first_ref[j], last_ref[j]
         here = pl.ds(pl.multiple_of(j * TILE, TILE), TILE)
@@ -230,16 +237,23 @@
         @pl.when(j == 0)
         def _():
             dq[...] = jnp.zeros(dq.shape, jnp.float32)
+            for ref in done_refs:
+                d_ref[...] = ref[...]
+            lane = lax.broadcasted_iota(jnp.int32, (TILE, half), 1)
             for b in range(blocks):
                 r, off = b * TILE // share, b * TILE % share
                 base = (place_ref[0] ^ r) * share + off
                 rows = pl.ds(pl.multiple_of(base, TILE), TILE)
+                sums = jnp.zeros((TILE, half), jnp.float32)
                 for h in range(heads):
-                    g = g_refs[r][off : off + TILE, h * HD : (h + 1) * HD]
+                    at = (head + h) * HD
+                    g = g_refs[r][off : off + TILE, at : at + HD]
                     split[h, rows, :] = g
                     dots = jnp.sum(g.astype(jnp.float32) * o_ref[h, rows, :], axis=1, keepdims=True)
-                    dots = jnp.transpose(jnp.broadcast_to(dots, (TILE, half)))
-                    inner[h, :, rows] = dots[0:1, :]
+                    sums = jnp.where(lane == h, dots, sums)
+                sums = jnp.transpose(sums)
+                for h in range(heads):
+                    inner[h, :, rows] = sums[h : h + 1, :]
 
         dk[...] = jnp.zeros(dk.shape, jnp.float32)
         dv[...] = jnp.zeros(dv.shape, jnp.float32)
@@ -259,13 +273,17 @@
             return carry
 
         lax.fori_loop(lo, hi, step, 0)
+        source = lax.broadcasted_iota(jnp.int32, (HD, HD), 0)
+        target = lax.broadcasted_iota(jnp.int32, (HD, HD), 1)
+        moves = (source == (target + HD // 2) % HD).astype(jnp.float32).astype(jnp.bfloat16)
         turn = jnp.transpose(t_ref[:, here])
         cosine, sine = turn[:, :HD], turn[:, HD:]
         for h in range(heads):
+            at = cols + (head + h) * HD
             w = dk[h]
-            w = (w * cosine - swap_halves(w) * sine).astype(jnp.bfloat16)
-            d_ref[here, cols + h * HD : cols + (h + 1) * HD] = w
-            d_ref[here, 2 * cols + h * HD : 2 * cols + (h + 1) * HD] = dv[h].astype(jnp.bfloat16)
+            w = w * cosine - nn_dot(w.astype(jnp.bfloat16), moves) * sine
+            d_ref[here, at : at + HD] = w.astype(jnp.bfloat16)
+            d_ref[here, cols + at : cols + at + HD] = dv[h].astype(jnp.bfloat16)
 
         @pl.when(j == blocks - 1)
         def _():
@@ -275,25 +293,27 @@
                 cosine, sine = turn[:, :HD], turn[:, HD:]
                 for h in range(heads):
                     w = dq[h, rows, :] * HD**-0.5
-                    w = w * cosine - swap_halves(w) * sine
-                    d_ref[rows, h * HD : (h + 1) * HD] = w.astype(jnp.bfloat16)
-
+                    w = w * cosine - nn_dot(w.astype(jnp.bfloat16), moves) * sine
+                    at = (head + h) * HD
+                    d_ref[rows, at : at + HD] = w.astype(jnp.bfloat16)
+
+    some = pl.BlockSpec((heads, tok_count, HD), lambda *_: (head // heads, 0, 0))
     return pl.pallas_call(
         body,
         grid_spec=pltpu.PrefetchScalarGridSpec(
             num_scalar_prefetch=3,
             grid=(blocks,),
             in_specs=[
-                whole(query.shape),
-                whole(key.shape),
-                whole(value.shape),
+                some,
+                some,
+                some,
                 pl.BlockSpec((TILE, half), lambda i, *_: (i, 0)),
                 whole(seg_row.shape),
-                whole(out.shape),
-                whole(lse.shape),
+                some,
+                pl.BlockSpec((heads, 1, tok_count), lambda *_: (head // heads, 0, 0)),
                 whole(tables.shape),
             ]
-            + [whole(g.shape) for g in grads],
+            + [whole(g.shape) for g in (*grads, *done)],
             out_specs=whole((tok_count, 3 * cols)),
             scratch_shapes=[
                 pltpu.VMEM((heads, tok_count, HD), jnp.bfloat16),
@@ -305,7 +325,7 @@
         ),
         out_shape=jax.ShapeDtypeStruct((tok_count, 3 * cols), jnp.bfloat16),
         name="attend_grad",
-    )(first, last, place, query, key, value, seg_col, seg_row, out, lse, tables, *grads)
+    )(first, last, place, query, key, value, seg_col, seg_row, out, lse, tables, *grads, *done)
 
 
 def swap(value, axis, step):
@@ -351,19 +371,18 @@
 
 def reduce_near(total, place):
     count = lax.axis_size("dp")
-    rows, cols = total.shape[0] // count, total.shape[1]
-    order = place[0] ^ jnp.array([*range(0, count, 2), *range(1, count, 2)], jnp.int32)
-    ranked = jnp.take(total.reshape(count, rows, cols), order, axis=0, mode="clip")
-    return ranked[: count // 2], swap(ranked[count // 2 :], "dp", 1)
+    blocks = total.reshape(count, total.shape[0] // count, total.shape[1])
+    near, far = (
+        jnp.take(blocks, place[0] ^ jnp.arange(k, count, 2), axis=0, mode="clip") for k in (0, 1)
+    )
+    return near, swap(far, "dp", 1)
 
 
 def reduce_far(near, come):
     near = near.astype(jnp.float32) + come.astype(jnp.float32)
     low = near.astype(jnp.bfloat16)
-    result = near[0]
-    for slot in range(1, near.shape[0]):
-        result = result + swap(low[slot], "dp", 2 * slot).astype(jnp.float32)
-    return result
+    come = [swap(low[slot], "dp", 2 * slot) for slot in range(1, near.shape[0])]
+    return near[0] + sum(part.astype(jnp.float32) for part in come)
 
 
 def layer(
@@ -597,31 +616,20 @@
     chip_sent, d_att = lax.optimization_barrier((chip_sent.astype(jnp.bfloat16), d_att))
     column_come = swap(chip_sent, "tensor", 2)
 
-    d_qkv = attend_grad(
-        first,
-        last,
-        place,
-        query,
-        key,
-        value,
-        seg_col,
-        seg_row,
-        d_att,
-        attended_wide,
-        log_total,
-        tables,
-    )
+    shared = (first, last, place, query, key, value, seg_col, seg_row)
+    shared = (*shared, d_att, attended_wide, log_total, tables)
+    d_qkv = attend_grad(*shared, 0, ())
+    d_qkv, column_come = lax.optimization_barrier((d_qkv, column_come))
+    column = grads_near[0].astype(jnp.float32) + grads_come[0].astype(jnp.float32)
+    column = (column + column_come.astype(jnp.float32)).astype(jnp.bfloat16)
+    column_near, column_come = reduce_near(column, dp_place)
+    d_qkv = attend_grad(*shared, heads_dev - 1, (d_qkv,))
     d_far = back_to_width(d_qkv, qkv_flat, place, (1, 3), share)
     d_near = back_to_width(d_qkv, qkv_flat, place, (0, 2), share)
     d_side = swap(d_far, "tensor", 1)
     d_sent = d_near[1].astype(jnp.float32) + d_side[1].astype(jnp.float32)
-    d_sent, d_qkv, column_come = lax.optimization_barrier(
-        (d_sent.astype(jnp.bfloat16), d_qkv, column_come)
-    )
+    d_sent, d_qkv = lax.optimization_barrier((d_sent.astype(jnp.bfloat16), d_qkv))
     d_come = swap(d_sent, "tensor", 2)
-    column = grads_near[0].astype(jnp.float32) + grads_come[0].astype(jnp.float32)
-    column = (column + column_come.astype(jnp.float32)).astype(jnp.bfloat16)
-    column_near, column_come = reduce_near(column, dp_place)
     qkv_total = jnp.einsum("td,tf->df", h_one, d_qkv, preferred_element_type=jnp.float32)
     qkv_near, qkv_come = reduce_near(qkv_total.astype(jnp.bfloat16), dp_place)
     normed_one, factor_one = normalize(my_tokens.astype(jnp.float32))

time: 411 us -> 388 us (0.944)
  waiting for transfers between devices: 143 us -> 107 us
  Pallas kernels: 152 us -> 162 us
  starting transfers between devices: 45.6 us -> 50.6 us
    ppermute x43, waiting for transfers between devices: 143 us -> 107 us  [swap(): return lax.ppermute(value, axis, [(i, i ^ step) for i in range(count)])]
    pallas_call x1 -> x2, Pallas kernels: 56.7 us -> 67.6 us  [attend_grad(): pl.pallas_call(body, grid_spec=pltpu.PrefetchScalarGridSpec(num_scalar_pr...]
    ppermute x43, starting transfers between devices: 45.6 us -> 50.6 us  [swap(): return lax.ppermute(value, axis, [(i, i ^ step) for i in range(count)])]
  transfers between devices with their start and end apart: 43 -> 43, of which waited for: 17 -> 19; matrix products, arithmetic and copies ran while one was open for 14% -> 13% of each run, Pallas kernels for 14% -> 25%
where the time goes in v2:
time: 388 us; the launch traced here: 381 us
  Pallas kernels  162 us (42%)
  waiting for transfers between devices  107 us (28%)
  starting transfers between devices  50.6 us (13%)
  other arithmetic  33 us (9%)
  local copies, waits for them, and re-layouts  24.4 us (6%)
    ppermute x43, waiting for transfers between devices, swap(): return lax.ppermute(value, axis, [(i, i ^ step) for i in range(count)])  107 us
    pallas_call x2, Pallas kernels, attend_grad(): pl.pallas_call(body, grid_spec=pltpu.PrefetchScalarGridSpec(num_scalar_pr...  67.6 us
    ppermute x43, starting transfers between devices, swap(): return lax.ppermute(value, axis, [(i, i ^ step) for i in range(count)])  50.6 us
    pallas_call x1, Pallas kernels, attend(): pl.pallas_call(body, grid_spec=pltpu.PrefetchScalarGridSpec(num_scalar_pr...  28.5 us
    pallas_call x1, Pallas kernels, layer(): pl.pallas_call(body, grid=(tok_count // rows,), in_specs=[tile(head_cols)...  19.4 us
    pallas_call x2, Pallas kernels, weight_grads(): pl.pallas_call(body, out_shape=jax.ShapeDtypeStruct((2, width, wide), jnp...  15.4 us
    pallas_call x4, Pallas kernels, assemble(): pl.pallas_call(body, grid_spec=pltpu.PrefetchScalarGridSpec(num_scalar_pr...  15.1 us
    pallas_call x1, Pallas kernels, project_heads(): pl.pallas_call(body, grid=(tok_count // rows,), in_specs=[pl.BlockSpec((r...  8.23 us
  transfers between devices with their start and end apart: 43, of which 19 were waited for; matrix products, arithmetic and copies ran while one was open for 13% of the time, Pallas kernels for 25%

profile of v2, /device:TPU:0, one launch (start us, length us, event | category | flops | bytes accessed | tf_op | source)
XLA Modules:
  0.0 381.1 jit_solution(6105566185122294959)
XLA Ops:
  2.0 5.1 %collective-permute-start.3 = (bf16[96,576]{1,0:T(8,128)(2,1)S(1)}, bf16[96,576]{1,0:T(8,128)(2,1)}, u32[]{:S(2)}, u32[]{:S(2)}) collective-permute-start(bf16[96,576]{1,0:T(8,128)(2,1)S(1)} %copy.56.refs_0_), channel_id=1, source_target_pairs={{0,24},{4,28},{8,16},{12,20},{16,8},{20,12},{24,0},{28,4},{1,25},{... | collective-permute-start | bytes 331784 | tf_op jit(solution)/shard_map/ppermute | solution.py:333
  27.9 2.9 collective-permute-start.5
  41.6 8.2 %project_heads.1 = (bf16[3,2048,64]{2,1,0:T(8,128)(2,1)}, bf16[3,2048,64]{2,1,0:T(8,128)(2,1)}, bf16[3,2048,64]{2,1,0:T(8,128)(2,1)}) custom-call(bf16[2048,768]{1,0:T(8,128)(2,1)} %fusion.4.h_ref, bf16[768,576]{1,0:T(8,128)(2,1)} %assemble.4.w_ref, f32[128,2048]{1,0:T(8,128)} %pad_maximum_fusion.t_ref), custom_call_target="tpu_custom_call" | custom-call | tf_op jit(solution)/shard_map/project_heads/pallas_call | solution.py:110
  49.9 11.2 %collective-permute-done.5.refs_4_ = bf16[2,96,1152]{2,1,0:T(8,128)(2,1)} collective-permute-done((bf16[2,96,1152]{2,1,0:T(8,128)(2,1)}, bf16[2,96,1152]{2,1,0:T(8,128)(2,1)}, u32[]{:S(2)}, u32[]{:S(2)}) %collective-permute-start.5) | collective-permute-done | bytes 442400 | tf_op jit(solution)/shard_map/ppermute | solution.py:333
  65.2 9.3 %collective-permute-done.14.refs_1_ = bf16[2,96,1152]{2,1,0:T(8,128)(2,1)} collective-permute-done((bf16[2,96,1152]{2,1,0:T(8,128)(2,1)}, bf16[2,96,1152]{2,1,0:T(8,128)(2,1)}, u32[]{:S(2)}, u32[]{:S(2)}) %collective-permute-start.14) | collective-permute-done | bytes 442400 | tf_op jit(solution)/shard_map/ppermute | solution.py:333
  74.5 9.5 %collective-permute-done.15.refs_3_ = bf16[2,96,1152]{2,1,0:T(8,128)(2,1)} collective-permute-done((bf16[2,96,1152]{2,1,0:T(8,128)(2,1)}, bf16[2,96,1152]{2,1,0:T(8,128)(2,1)}, u32[]{:S(2)}, u32[]{:S(2)}) %collective-permute-start.15) | collective-permute-done | bytes 442400 | tf_op jit(solution)/shard_map/ppermute | solution.py:333
  83.9 7.7 %collective-permute-done.16.refs_5_ = bf16[2,96,1152]{2,1,0:T(8,128)(2,1)} collective-permute-done((bf16[2,96,1152]{2,1,0:T(8,128)(2,1)}, bf16[2,96,1152]{2,1,0:T(8,128)(2,1)}, u32[]{:S(2)}, u32[]{:S(2)}) %collective-permute-start.16) | collective-permute-done | bytes 442400 | tf_op jit(solution)/shard_map/ppermute | solution.py:333
  91.7 4.7 %collective-permute-done.17.refs_7_ = bf16[2,96,1152]{2,1,0:T(8,128)(2,1)} collective-permute-done((bf16[2,96,1152]{2,1,0:T(8,128)(2,1)}, bf16[2,96,1152]{2,1,0:T(8,128)(2,1)}, u32[]{:S(2)}, u32[]{:S(2)}) %collective-permute-start.17) | collective-permute-done | bytes 442400 | tf_op jit(solution)/shard_map/ppermute | solution.py:333
  96.4 4.0 %assemble.5.refs_7_ = bf16[2,768,1152]{2,1,0:T(8,128)(2,1)} custom-call(s32[1]{0:T(128)} %bitcast.8.place_ref, bf16[2,96,1152]{2,1,0:T(8,128)(2,1)} %pad_maximum_fusion.1.refs_0_, bf16[2,96,1152]{2,1,0:T(8,128)(2,1)} %collective-permute-done.14.refs_1_, bf16[2,96,1152]{2,1,0:T(8,128)(2,1)} %collective-permute-done.4.refs_2_, ...), custom_call_target="tpu_custom_call" | custom-call | tf_op jit(solution)/shard_map/assemble/pallas_call | solution.py:359
  102.5 28.5 %attend.1 = (bf16[512,192]{1,0:T(8,128)(2,1)}, bf16[512,192]{1,0:T(8,128)(2,1)}, bf16[512,192]{1,0:T(8,128)(2,1)}, bf16[512,192]{1,0:T(8,128)(2,1)}, f32[3,2048,64]{2,1,0:T(8,128)}, /*index=5*/f32[3,1,2048]{2,1,0:T(1,128)}) custom-call(s32[8]{0:T(128)} %get-tuple-element.144.first_ref, s32[8]{0:T(128)} %get-tuple-element.143.last_ref, s32[1]{0:T(128)} %bitcast.place_ref, ...), custom_call_target="tpu_custom_call" | custom-call | tf_op jit(solution)/shard_map/attend/pallas_call | solution.py:182
  136.8 4.2 %collective-permute-done.12.refs_2_.b_ref = bf16[512,192]{1,0:T(8,128)(2,1)S(1)} collective-permute-done((bf16[512,192]{1,0:T(8,128)(2,1)}, bf16[512,192]{1,0:T(8,128)(2,1)S(1)}, u32[]{:S(2)}, u32[]{:S(2)}) %collective-permute-start.12) | collective-permute-done | bytes 196640 | tf_op jit(solution)/shard_map/ppermute | solution.py:333
  141.0 3.8 %collective-permute-done.13.refs_3_.b_ref = bf16[512,192]{1,0:T(8,128)(2,1)S(1)} collective-permute-done((bf16[512,192]{1,0:T(8,128)(2,1)}, bf16[512,192]{1,0:T(8,128)(2,1)S(1)}, u32[]{:S(2)}, u32[]{:S(2)}) %collective-permute-start.13) | collective-permute-done | bytes 196640 | tf_op jit(solution)/shard_map/ppermute | solution.py:333
  145.5 19.4 %layer.1 = (bf16[512,768]{1,0:T(8,128)(2,1)}, f32[512,768]{1,0:T(8,128)}, bf16[512,768]{1,0:T(8,128)(2,1)}, bf16[512,768]{1,0:T(8,128)(2,1)}, bf16[512,1152]{1,0...) custom-call(bf16[512,192]{1,0:T(8,128)(2,1)} %get-tuple-element.57.r, ...), custom_call_target="tpu_custom_call" | custom-call | tf_op jit(solution)/shard_map/layer/pallas_call | solution.py:459
  165.0 8.0 %weight_grads.3 = bf16[2,768,1152]{2,1,0:T(8,128)(2,1)} custom-call(bf16[512,768]{1,0:T(8,128)(2,1)} %get-tuple-element.69.h_ref, bf16[512,1152]{1,0:T(8,128)(2,1)} %get-tuple-element.70.f_ref, bf16[512,1152]{1,0:T(8,128)(2,1)} %get-tuple-element.71.s_ref, bf16[512,768]{1,0:T(8,128)(2,1)} %constant_dynamic-slice_fusion.refs_5_.c_ref, ...), custom_call_target="tpu_custom_call" | custom-call | tf_op jit(solution)/shard_map/weight_grads/pallas_call | solution.py:516
  175.6 7.4 %weight_grads.2 = bf16[2,768,1152]{2,1,0:T(8,128)(2,1)} custom-call(bf16[512,768]{1,0:T(8,128)(2,1)} %get-tuple-element.69.h_ref, bf16[512,1152]{1,0:T(8,128)(2,1)} %get-tuple-element.70.f_ref, bf16[512,1152]{1,0:T(8,128)(2,1)} %get-tuple-element.71.s_ref, bf16[512,768]{1,0:T(8,128)(2,1)} %constant_dynamic-slice_fusion.refs_5_.c_ref, ...), custom_call_target="tpu_custom_call" | custom-call | tf_op jit(solution)/shard_map/weight_grads/pallas_call | solution.py:516
  183.0 3.7 fusion.10
  188.3 40.0 %attend_grad.2.refs_4_ = bf16[2048,576]{1,0:T(8,128)(2,1)} custom-call(s32[8]{0:T(128)} %get-tuple-element.144.first_ref, s32[8]{0:T(128)} %get-tuple-element.143.last_ref, s32[1]{0:T(128)} %bitcast.place_ref, bf16[3,2048,64]{2,1,0:T(8,128)(2,1)} %get-tuple-element.54.q_ref, bf16[3,2048,64]{2,1,0:T(8,128)(2,1)} %get-tuple-element.55.k_ref, ...), custom_call_target="tpu_custom_call" | custom-call | tf_op jit(solution)/shard_map/attend_grad/pallas_call | solution.py:301
  228.7 27.6 %attend_grad.3.d_ref = bf16[2048,576]{1,0:T(8,128)(2,1)} custom-call(s32[8]{0:T(128)} %get-tuple-element.144.first_ref, s32[8]{0:T(128)} %get-tuple-element.143.last_ref, s32[1]{0:T(128)} %bitcast.place_ref, bf16[3,2048,64]{2,1,0:T(8,128)(2,1)} %get-tuple-element.54.q_ref, bf16[3,2048,64]{2,1,0:T(8,128)(2,1)} %get-tuple-element.55.k_ref, ...), custom_call_target="tpu_custom_call" | custom-call | tf_op jit(solution)/shard_map/attend_grad/pallas_call | solution.py:301
  256.3 3.9 %back_to_width.3 = bf16[2,512,768]{2,1,0:T(8,128)(2,1)} custom-call(s32[1]{0:T(128)} %bitcast.place_ref, bf16[2048,576]{1,0:T(8,128)(2,1)} %attend_grad.3.d_ref, bf16[768,576]{1,0:T(8,128)(2,1)} %assemble.4.w_ref), custom_call_target="tpu_custom_call" | custom-call | tf_op jit(solution)/shard_map/back_to_width/pallas_call | solution.py:530
  260.2 3.2 fusion.5
  266.7 18.6 %collective-permute-done.20.refs_2_ = bf16[512,768]{1,0:T(8,128)(2,1)} collective-permute-done((bf16[512,768]{1,0:T(8,128)(2,1)}, bf16[512,768]{1,0:T(8,128)(2,1)}, u32[]{:S(2)}, u32[]{:S(2)}) %collective-permute-start.20) | collective-permute-done | bytes 786464 | tf_op jit(solution)/shard_map/ppermute | solution.py:333
  285.2 4.0 %back_to_width.2 = bf16[2,512,768]{2,1,0:T(8,128)(2,1)} custom-call(s32[1]{0:T(128)} %bitcast.place_ref, bf16[2048,576]{1,0:T(8,128)(2,1)} %attend_grad.3.d_ref, bf16[768,576]{1,0:T(8,128)(2,1)} %assemble.4.w_ref), custom_call_target="tpu_custom_call" | custom-call | tf_op jit(solution)/shard_map/back_to_width/pallas_call | solution.py:530
  290.8 3.0 fusion.24
  297.8 8.8 %collective-permute-start.40 = (bf16[96,1152]{1,0:T(8,128)(2,1)}, bf16[96,1152]{1,0:T(8,128)(2,1)S(1)}, u32[]{:S(2)}, u32[]{:S(2)}) collective-permute-start(bf16[96,1152]{1,0:T(8,128)(2,1)} %get-tuple-element.134), channel_id=1, source_target_pairs={{0,8},{4,12},{8,0},{12,4},{16,24},{20,28},{24,16},{28,20},{1,9},{5... | collective-permute-start | bytes 663560 | tf_op jit(solution)/shard_map/ppermute | solution.py:333
  309.0 3.7 assemble.6
  312.8 4.0 %collective-permute-done.40 = bf16[96,1152]{1,0:T(8,128)(2,1)S(1)} collective-permute-done((bf16[96,1152]{1,0:T(8,128)(2,1)}, bf16[96,1152]{1,0:T(8,128)(2,1)S(1)}, u32[]{:S(2)}, u32[]{:S(2)}) %collective-permute-start.40) | collective-permute-done | bytes 221216 | tf_op jit(solution)/shard_map/ppermute | solution.py:333
  316.8 8.7 %collective-permute-done.41 = bf16[96,1152]{1,0:T(8,128)(2,1)S(1)} collective-permute-done((bf16[96,1152]{1,0:T(8,128)(2,1)}, bf16[96,1152]{1,0:T(8,128)(2,1)S(1)}, u32[]{:S(2)}, u32[]{:S(2)}) %collective-permute-start.41) | collective-permute-done | bytes 221216 | tf_op jit(solution)/shard_map/ppermute | solution.py:333
  331.4 3.2 fusion.15.refs_0_
  341.8 8.8 %collective-permute-done.32 = bf16[4,96,576]{2,1,0:T(8,128)(2,1)S(1)} collective-permute-done((bf16[4,96,576]{2,1,0:T(8,128)(2,1)S(1)}, bf16[4,96,576]{2,1,0:T(8,128)(2,1)S(1)}, u32[]{:S(2)}, u32[]{:S(2)}) %collective-permute-start.32) | collective-permute-done | bytes 442400 | tf_op jit(solution)/shard_map/ppermute | solution.py:333
  352.5 5.4 %collective-permute-start.33 = (bf16[96,576]{1,0:T(8,128)(2,1)S(1)}, bf16[96,576]{1,0:T(8,128)(2,1)S(1)}, u32[]{:S(2)}, u32[]{:S(2)}) collective-permute-start(bf16[96,576]{1,0:T(8,128)(2,1)S(1)} %get-tuple-element.137), channel_id=1, source_target_pairs={{0,8},{4,12},{8,0},{12,4},{16,24},{20,28},{24,16},{28,20},{1,9},{5... | collective-permute-start | bytes 331784 | tf_op jit(solution)/shard_map/ppermute | solution.py:333
  363.9 6.5 %collective-permute-done.34 = bf16[96,576]{1,0:T(8,128)(2,1)S(1)} collective-permute-done((bf16[96,576]{1,0:T(8,128)(2,1)S(1)}, bf16[96,576]{1,0:T(8,128)(2,1)S(1)}, u32[]{:S(2)}, u32[]{:S(2)}) %collective-permute-start.34) | collective-permute-done | bytes 110624 | tf_op jit(solution)/shard_map/ppermute | solution.py:333
  375.7 5.1 %assemble.7 = f32[2048,768]{1,0:T(8,128)} custom-call(s32[1]{0:T(128)} %bitcast.place_ref, bf16[512,768]{1,0:T(8,128)(2,1)} %fusion.15.refs_0_, bf16[512,768]{1,0:T(8,128)(2,1)} %collective-permute-done.29.refs_1_, bf16[512,768]{1,0:T(8,128)(2,1)} %collective-permute-done.30.refs_2_, bf16[512,768]{1,0:T(8,128)(2,1)} %collective-permute-done.31.refs_3_), custom_call_target="tpu_custom_call" | custom-call | tf_op jit(solution)/shard_map/assemble/pallas_call | solution.py:359
  (192 shorter events, 87.4 us)
Async XLA Ops:
  2.0 22.2 %collective-permute-start.3 = (bf16[96,576]{1,0:T(8,128)(2,1)S(1)}, bf16[96,576]{1,0:T(8,128)(2,1)}, u32[]{:S(2)}, u32[]{:S(2)}) collective-permute-start(bf16[96,576]{1,0:T(8,128)(2,1)S(1)} %copy.56.refs_0_), channel_id=1, source_target_pairs={{0,24},{4,28},{8,16},{12,20},{16,8},{20,12},{24,0},{28,4},{1,25},{... | collective-permute-start | bytes 331784 | tf_op jit(solution)/shard_map/ppermute | solution.py:333
  7.2 19.4 %collective-permute-start.1 = (bf16[96,576]{1,0:T(8,128)(2,1)S(1)}, bf16[96,576]{1,0:T(8,128)(2,1)}, u32[]{:S(2)}, u32[]{:S(2)}) collective-permute-start(bf16[96,576]{1,0:T(8,128)(2,1)S(1)} %copy.56.refs_0_), channel_id=1, source_target_pairs={{0,8},{4,12},{8,0},{12,4},{16,24},{20,28},{24,16},{28,20},{1,9},{5... | collective-permute-start | bytes 331784 | tf_op jit(solution)/shard_map/ppermute | solution.py:333
  7.2 19.4 %collective-permute-start.2 = (bf16[96,576]{1,0:T(8,128)(2,1)S(1)}, bf16[96,576]{1,0:T(8,128)(2,1)}, u32[]{:S(2)}, u32[]{:S(2)}) collective-permute-start(bf16[96,576]{1,0:T(8,128)(2,1)S(1)} %copy.56.refs_0_), channel_id=1, source_target_pairs={{0,16},{4,20},{8,24},{12,28},{16,0},{20,4},{24,8},{28,12},{1,17},{... | collective-permute-start | bytes 331784 | tf_op jit(solution)/shard_map/ppermute | solution.py:333
  7.8 24.2 %collective-permute-start.7 = (bf16[96,576]{1,0:T(8,128)(2,1)S(1)}, bf16[96,576]{1,0:T(8,128)(2,1)}, u32[]{:S(2)}, u32[]{:S(2)}) collective-permute-start(bf16[96,576]{1,0:T(8,128)(2,1)S(1)} %copy.56.refs_0_), channel_id=1, source_target_pairs={{0,4},{4,0},{8,12},{12,8},{16,20},{20,16},{24,28},{28,24},{1,5},{5... | collective-permute-start | bytes 331784 | tf_op jit(solution)/shard_map/ppermute | solution.py:333
  26.6 23.3 %collective-permute-start.4 = (bf16[2,96,1152]{2,1,0:T(8,128)(2,1)}, bf16[2,96,1152]{2,1,0:T(8,128)(2,1)}, u32[]{:S(2)}, u32[]{:S(2)}) collective-permute-start(bf16[2,96,1152]{2,1,0:T(8,128)(2,1)} %pad_maximum_fusion.1.refs_0_), channel_id=1, source_target_pairs={{0,8},{4,12},{8,0},{12,4},{16,24},{20,28},{24,16},{28,20},{1,9},{5... | collective-permute-start | bytes 1327112 | tf_op jit(solution)/shard_map/ppermute | solution.py:333
  27.9 33.2 %collective-permute-start.5 = (bf16[2,96,1152]{2,1,0:T(8,128)(2,1)}, bf16[2,96,1152]{2,1,0:T(8,128)(2,1)}, u32[]{:S(2)}, u32[]{:S(2)}) collective-permute-start(bf16[2,96,1152]{2,1,0:T(8,128)(2,1)} %pad_maximum_fusion.1.refs_0_), channel_id=1, source_target_pairs={{0,16},{4,20},{8,24},{12,28},{16,0},{20,4},{24,8},{28,12},{1,17},{... | collective-permute-start | bytes 1327112 | tf_op jit(solution)/shard_map/ppermute | solution.py:333
  30.8 30.3 %collective-permute-start.6 = (bf16[2,96,1152]{2,1,0:T(8,128)(2,1)}, bf16[2,96,1152]{2,1,0:T(8,128)(2,1)}, u32[]{:S(2)}, u32[]{:S(2)}) collective-permute-start(bf16[2,96,1152]{2,1,0:T(8,128)(2,1)} %pad_maximum_fusion.1.refs_0_), channel_id=1, source_target_pairs={{0,24},{4,28},{8,16},{12,20},{16,8},{20,12},{24,0},{28,4},{1,25},{... | collective-permute-start | bytes 1327112 | tf_op jit(solution)/shard_map/ppermute | solution.py:333
  61.1 13.4 %collective-permute-start.14 = (bf16[2,96,1152]{2,1,0:T(8,128)(2,1)}, bf16[2,96,1152]{2,1,0:T(8,128)(2,1)}, u32[]{:S(2)}, u32[]{:S(2)}) collective-permute-start(bf16[2,96,1152]{2,1,0:T(8,128)(2,1)} %pad_maximum_fusion.1.refs_0_), channel_id=1, source_target_pairs={{0,4},{4,0},{8,12},{12,8},{16,20},{20,16},{24,28},{28,24},{1,5},{5... | collective-permute-start | bytes 1327112 | tf_op jit(solution)/shard_map/ppermute | solution.py:333
  62.6 21.3 %collective-permute-start.15 = (bf16[2,96,1152]{2,1,0:T(8,128)(2,1)}, bf16[2,96,1152]{2,1,0:T(8,128)(2,1)}, u32[]{:S(2)}, u32[]{:S(2)}) collective-permute-start(bf16[2,96,1152]{2,1,0:T(8,128)(2,1)} %collective-permute-done.4.refs_2_), channel_id=1, source_target_pairs={{0,4},{4,0},{8,12},{12,8},{16,20},{20,16},{24,28},{28,24},{1,5},{5... | collective-permute-start | bytes 1327112 | tf_op jit(solution)/shard_map/ppermute | solution.py:333
  63.1 28.5 %collective-permute-start.16 = (bf16[2,96,1152]{2,1,0:T(8,128)(2,1)}, bf16[2,96,1152]{2,1,0:T(8,128)(2,1)}, u32[]{:S(2)}, u32[]{:S(2)}) collective-permute-start(bf16[2,96,1152]{2,1,0:T(8,128)(2,1)} %collective-permute-done.5.refs_4_), channel_id=1, source_target_pairs={{0,4},{4,0},{8,12},{12,8},{16,20},{20,16},{24,28},{28,24},{1,5},{5... | collective-permute-start | bytes 1327112 | tf_op jit(solution)/shard_map/ppermute | solution.py:333
  64.7 31.8 %collective-permute-start.17 = (bf16[2,96,1152]{2,1,0:T(8,128)(2,1)}, bf16[2,96,1152]{2,1,0:T(8,128)(2,1)}, u32[]{:S(2)}, u32[]{:S(2)}) collective-permute-start(bf16[2,96,1152]{2,1,0:T(8,128)(2,1)} %collective-permute-done.6.refs_6_), channel_id=1, source_target_pairs={{0,4},{4,0},{8,12},{12,8},{16,20},{20,16},{24,28},{28,24},{1,5},{5... | collective-permute-start | bytes 1327112 | tf_op jit(solution)/shard_map/ppermute | solution.py:333
  100.4 45.1 %collective-permute-start.18 = (bf16[2,768,1152]{2,1,0:T(8,128)(2,1)}, bf16[2,768,1152]{2,1,0:T(8,128)(2,1)}, u32[]{:S(2)}, u32[]{:S(2)}) collective-permute-start(bf16[2,768,1152]{2,1,0:T(8,128)(2,1)} %assemble.5.refs_7_), channel_id=1, source_target_pairs={{0,1},{1,0},{2,3},{3,2},{4,5},{5,4},{6,7},{7,6},{8,9},{9,8},{10,11... | collective-permute-start | bytes 10616840 | tf_op jit(solution)/shard_map/ppermute | solution.py:333
  132.1 12.7 %collective-permute-start.13 = (bf16[512,192]{1,0:T(8,128)(2,1)}, bf16[512,192]{1,0:T(8,128)(2,1)S(1)}, u32[]{:S(2)}, u32[]{:S(2)}) collective-permute-start(bf16[512,192]{1,0:T(8,128)(2,1)} %get-tuple-element.60), channel_id=1, source_target_pairs={{0,3},{1,2},{2,1},{3,0},{4,7},{5,6},{6,5},{7,4},{8,11},{9,10},{10,... | collective-permute-start | bytes 589832 | tf_op jit(solution)/shard_map/ppermute | solution.py:333
  173.8 12.9 %collective-permute-start.23 = (bf16[512,192]{1,0:T(8,128)(2,1)S(1)}, bf16[512,192]{1,0:T(8,128)(2,1)S(1)}, u32[]{:S(2)}, u32[]{:S(2)}) collective-permute-start(bf16[512,192]{1,0:T(8,128)(2,1)S(1)} %copy-done.29), channel_id=1, source_target_pairs={{0,1},{1,0},{2,3},{3,2},{4,5},{5,4},{6,7},{7,6},{8,9},{9,8},{10,11... | collective-permute-start | bytes 589832 | tf_op jit(solution)/shard_map/ppermute | solution.py:333
  173.8 12.9 %collective-permute-start.24 = (bf16[512,192]{1,0:T(8,128)(2,1)S(1)}, bf16[512,192]{1,0:T(8,128)(2,1)S(1)}, u32[]{:S(2)}, u32[]{:S(2)}) collective-permute-start(bf16[512,192]{1,0:T(8,128)(2,1)S(1)} %copy-done.28), channel_id=1, source_target_pairs={{0,2},{1,3},{2,0},{3,1},{4,6},{5,7},{6,4},{7,5},{8,10},{9,11},{10,... | collective-permute-start | bytes 589832 | tf_op jit(solution)/shard_map/ppermute | solution.py:333
  174.4 13.2 %collective-permute-start.25 = (bf16[512,192]{1,0:T(8,128)(2,1)S(1)}, bf16[512,192]{1,0:T(8,128)(2,1)S(1)}, u32[]{:S(2)}, u32[]{:S(2)}) collective-permute-start(bf16[512,192]{1,0:T(8,128)(2,1)S(1)} %copy-done.27), channel_id=1, source_target_pairs={{0,3},{1,2},{2,1},{3,0},{4,7},{5,6},{6,5},{7,4},{8,11},{9,10},{10,... | collective-permute-start | bytes 589832 | tf_op jit(solution)/shard_map/ppermute | solution.py:333
  187.6 41.1 %collective-permute-start.26 = (bf16[768,1152]{1,0:T(8,128)(2,1)}, bf16[768,1152]{1,0:T(8,128)(2,1)S(1)}, u32[]{:S(2)}, u32[]{:S(2)}) collective-permute-start(bf16[768,1152]{1,0:T(8,128)(2,1)} %fusion.10), channel_id=1, source_target_pairs={{0,2},{1,3},{2,0},{3,1},{4,6},{5,7},{6,4},{7,5},{8,10},{9,11},{10,... | collective-permute-start | bytes 5308424 | tf_op jit(solution)/shard_map/ppermute | solution.py:333
  260.2 33.5 %collective-permute-start.27 = (bf16[2,512,768]{2,1,0:T(8,128)(2,1)}, bf16[2,512,768]{2,1,0:T(8,128)(2,1)}, u32[]{:S(2)}, u32[]{:S(2)}) collective-permute-start(bf16[2,512,768]{2,1,0:T(8,128)(2,1)} %back_to_width.3), channel_id=1, source_target_pairs={{0,1},{1,0},{2,3},{3,2},{4,5},{5,4},{6,7},{7,6},{8,9},{9,8},{10,11... | collective-permute-start | bytes 4718600 | tf_op jit(solution)/shard_map/ppermute | solution.py:333
  265.0 25.8 %collective-permute-start.39 = (bf16[4,96,1152]{2,1,0:T(8,128)(2,1)}, bf16[4,96,1152]{2,1,0:T(8,128)(2,1)}, u32[]{:S(2)}, u32[]{:S(2)}) collective-permute-start(bf16[4,96,1152]{2,1,0:T(8,128)(2,1)} %gather_fusion.3), channel_id=1, source_target_pairs={{0,4},{4,0},{8,12},{12,8},{16,20},{20,16},{24,28},{28,24},{1,5},{5... | collective-permute-start | bytes 2654216 | tf_op jit(solution)/shard_map/ppermute | solution.py:333
  265.0 20.3 %collective-permute-start.20 = (bf16[512,768]{1,0:T(8,128)(2,1)}, bf16[512,768]{1,0:T(8,128)(2,1)}, u32[]{:S(2)}, u32[]{:S(2)}) collective-permute-start(bf16[512,768]{1,0:T(8,128)(2,1)} %get-tuple-element.65.refs_0_), channel_id=1, source_target_pairs={{0,2},{1,3},{2,0},{3,1},{4,6},{5,7},{6,4},{7,5},{8,10},{9,11},{10,... | collective-permute-start | bytes 2359304 | tf_op jit(solution)/shard_map/ppermute | solution.py:333
  266.5 41.1 %collective-permute-start.19 = (bf16[512,768]{1,0:T(8,128)(2,1)}, bf16[512,768]{1,0:T(8,128)(2,1)}, u32[]{:S(2)}, u32[]{:S(2)}) collective-permute-start(bf16[512,768]{1,0:T(8,128)(2,1)} %get-tuple-element.65.refs_0_), channel_id=1, source_target_pairs={{0,1},{1,0},{2,3},{3,2},{4,5},{5,4},{6,7},{7,6},{8,9},{9,8},{10,11... | collective-permute-start | bytes 2359304 | tf_op jit(solution)/shard_map/ppermute | solution.py:333
  285.2 23.8 %collective-permute-start.21 = (bf16[512,768]{1,0:T(8,128)(2,1)}, bf16[512,768]{1,0:T(8,128)(2,1)}, u32[]{:S(2)}, u32[]{:S(2)}) collective-permute-start(bf16[512,768]{1,0:T(8,128)(2,1)} %collective-permute-done.20.refs_2_), channel_id=1, source_target_pairs={{0,1},{1,0},{2,3},{3,2},{4,5},{5,4},{6,7},{7,6},{8,9},{9,8},{10,11... | collective-permute-start | bytes 2359304 | tf_op jit(solution)/shard_map/ppermute | solution.py:333
  296.0 33.1 %collective-permute-start.28 = (bf16[512,768]{1,0:T(8,128)(2,1)}, bf16[512,768]{1,0:T(8,128)(2,1)}, u32[]{:S(2)}, u32[]{:S(2)}) collective-permute-start(bf16[512,768]{1,0:T(8,128)(2,1)} %fusion.18), channel_id=1, source_target_pairs={{0,2},{1,3},{2,0},{3,1},{4,6},{5,7},{6,4},{7,5},{8,10},{9,11},{10,... | collective-permute-start | bytes 2359304 | tf_op jit(solution)/shard_map/ppermute | solution.py:333
  297.8 19.0 %collective-permute-start.40 = (bf16[96,1152]{1,0:T(8,128)(2,1)}, bf16[96,1152]{1,0:T(8,128)(2,1)S(1)}, u32[]{:S(2)}, u32[]{:S(2)}) collective-permute-start(bf16[96,1152]{1,0:T(8,128)(2,1)} %get-tuple-element.134), channel_id=1, source_target_pairs={{0,8},{4,12},{8,0},{12,4},{16,24},{20,28},{24,16},{28,20},{1,9},{5... | collective-permute-start | bytes 663560 | tf_op jit(solution)/shard_map/ppermute | solution.py:333
  306.6 18.9 %collective-permute-start.41 = (bf16[96,1152]{1,0:T(8,128)(2,1)}, bf16[96,1152]{1,0:T(8,128)(2,1)S(1)}, u32[]{:S(2)}, u32[]{:S(2)}) collective-permute-start(bf16[96,1152]{1,0:T(8,128)(2,1)} %get-tuple-element.136), channel_id=1, source_target_pairs={{0,16},{4,20},{8,24},{12,28},{16,0},{20,4},{24,8},{28,12},{1,17},{... | collective-permute-start | bytes 663560 | tf_op jit(solution)/shard_map/ppermute | solution.py:333
  307.6 18.0 %collective-permute-start.42 = (bf16[96,1152]{1,0:T(8,128)(2,1)S(1)}, bf16[96,1152]{1,0:T(8,128)(2,1)S(1)}, u32[]{:S(2)}, u32[]{:S(2)}) collective-permute-start(bf16[96,1152]{1,0:T(8,128)(2,1)S(1)} %get-tuple-element.135), channel_id=1, source_target_pairs={{0,24},{4,28},{8,16},{12,20},{16,8},{20,12},{24,0},{28,4},{1,25},{... | collective-permute-start | bytes 663560 | tf_op jit(solution)/shard_map/ppermute | solution.py:333
  334.6 17.9 %collective-permute-start.30 = (bf16[512,768]{1,0:T(8,128)(2,1)}, bf16[512,768]{1,0:T(8,128)(2,1)}, u32[]{:S(2)}, u32[]{:S(2)}) collective-permute-start(bf16[512,768]{1,0:T(8,128)(2,1)} %fusion.15.refs_0_), channel_id=1, source_target_pairs={{0,2},{1,3},{2,0},{3,1},{4,6},{5,7},{6,4},{7,5},{8,10},{9,11},{10,... | collective-permute-start | bytes 2359304 | tf_op jit(solution)/shard_map/ppermute | solution.py:333
  350.7 25.0 %collective-permute-start.29 = (bf16[512,768]{1,0:T(8,128)(2,1)}, bf16[512,768]{1,0:T(8,128)(2,1)}, u32[]{:S(2)}, u32[]{:S(2)}) collective-permute-start(bf16[512,768]{1,0:T(8,128)(2,1)} %fusion.15.refs_0_), channel_id=1, source_target_pairs={{0,1},{1,0},{2,3},{3,2},{4,5},{5,4},{6,7},{7,6},{8,9},{9,8},{10,11... | collective-permute-start | bytes 2359304 | tf_op jit(solution)/shard_map/ppermute | solution.py:333
  352.5 23.2 %collective-permute-start.31 = (bf16[512,768]{1,0:T(8,128)(2,1)}, bf16[512,768]{1,0:T(8,128)(2,1)}, u32[]{:S(2)}, u32[]{:S(2)}) collective-permute-start(bf16[512,768]{1,0:T(8,128)(2,1)} %collective-permute-done.30.refs_2_), channel_id=1, source_target_pairs={{0,1},{1,0},{2,3},{3,2},{4,5},{5,4},{6,7},{7,6},{8,9},{9,8},{10,11... | collective-permute-start | bytes 2359304 | tf_op jit(solution)/shard_map/ppermute | solution.py:333
  352.5 11.3 %collective-permute-start.33 = (bf16[96,576]{1,0:T(8,128)(2,1)S(1)}, bf16[96,576]{1,0:T(8,128)(2,1)S(1)}, u32[]{:S(2)}, u32[]{:S(2)}) collective-permute-start(bf16[96,576]{1,0:T(8,128)(2,1)S(1)} %get-tuple-element.137), channel_id=1, source_target_pairs={{0,8},{4,12},{8,0},{12,4},{16,24},{20,28},{24,16},{28,20},{1,9},{5... | collective-permute-start | bytes 331784 | tf_op jit(solution)/shard_map/ppermute | solution.py:333
  357.9 12.4 %collective-permute-start.34 = (bf16[96,576]{1,0:T(8,128)(2,1)S(1)}, bf16[96,576]{1,0:T(8,128)(2,1)S(1)}, u32[]{:S(2)}, u32[]{:S(2)}) collective-permute-start(bf16[96,576]{1,0:T(8,128)(2,1)S(1)} %get-tuple-element.139), channel_id=1, source_target_pairs={{0,16},{4,20},{8,24},{12,28},{16,0},{20,4},{24,8},{28,12},{1,17},{... | collective-permute-start | bytes 331784 | tf_op jit(solution)/shard_map/ppermute | solution.py:333
  358.9 11.4 %collective-permute-start.35 = (bf16[96,576]{1,0:T(8,128)(2,1)S(1)}, bf16[96,576]{1,0:T(8,128)(2,1)S(1)}, u32[]{:S(2)}, u32[]{:S(2)}) collective-permute-start(bf16[96,576]{1,0:T(8,128)(2,1)S(1)} %get-tuple-element.138), channel_id=1, source_target_pairs={{0,24},{4,28},{8,16},{12,20},{16,8},{20,12},{24,0},{28,4},{1,25},{... | collective-permute-start | bytes 331784 | tf_op jit(solution)/shard_map/ppermute | solution.py:333
  (41 other events, 475.6 us)
